TPU v7x, 32 devices: a whole 2x2x4 slice. The times are simulated.
32 devices in a mesh: band: 8 (over y, x, core), lev: 4 (over z).
Axes of the slice: x: 2, y: 2, z: 4, core: 2. Of those that a mesh axis runs over, the one named last changes fastest.
Arguments:
- spectral: bfloat16 [2, 2, 4, 1280, 2561], P(None, None, 'lev', 'band'), may hold values from -0.005859375 to 0.005859375
- legendre: bfloat16 [1280, 8, 2561], P('band'), may hold values from -6 to 6
- cycle_len: int32 [8], replicated, may hold values from 20 to 10256, as said below
- pair_wave: int32 [1280], replicated, may hold values from 0 to 1279, each once
- quad_weight: float32 [8], replicated, may hold values from 2 to 20
- forcing: bfloat16 [2, 4, 8, 10256], P(None, None, 'band', 'lev'), may hold values from -6 to 6
- mixing: bfloat16 [2, 4, 4], replicated, may hold values from -3 to 3
Outputs:
- tendency: bfloat16 [2, 2, 4, 1280, 2561], P(None, None, 'lev', 'band')
Inputs may be any that keep to these rules, and one draw needn't show every extreme that they name: `cycle_len`: each length is 20 + 4 i for distinct cycle numbers i from 0 to 2559; the cycle of length 10256 is present in every draw. `pair_wave`: each number from 0 to 1279 appears once.
All inputs are finite; a program needn't handle non-finite values.
Results may differ from a plain program's by a relative error of at most 0.008.
Values may be sent and summed in bfloat16 or wider, within the bound.
A program may use at most 128 MiB of HBM per device.

v0:
```python
import jax
import jax.numpy as jnp
from jax import lax
from jax.sharding import PartitionSpec as P

TRUNC = 2559
FIELDS = 2


TWO_PI = 6.283185307179586


def phases(numerator, length_value):
    residue = numerator % length_value
    angles = residue.astype(jnp.float32) * (TWO_PI / length_value.astype(jnp.float32))
    return (jnp.cos(angles), jnp.sin(angles))


def on_device(spectral, legendre, cycle_len, pair_wave, quad_weight, forcing, mixing):
    band_count = lax.axis_size("band")
    lev_count = lax.axis_size("lev")
    band_id = lax.axis_index("band")
    lev_id = lax.axis_index("lev")
    lev_dev = spectral.shape[2]
    pair_dev = spectral.shape[3]
    packed = spectral.shape[4]
    cycle_count = legendre.shape[1]
    levels = forcing.shape[1]
    device_cycle_index = forcing.shape[2]
    points_dev = forcing.shape[3]
    waves_total = TRUNC + 1
    stacked_rows = 4 * FIELDS * lev_dev
    my_low = lax.dynamic_slice_in_dim(pair_wave, band_id * pair_dev, pair_dev)
    column = jnp.arange(packed, dtype=jnp.int32)
    lower_part = column[None, :] < (waves_total - my_low)[:, None]
    spec_rows = jnp.transpose(spectral, (3, 0, 1, 2, 4))
    lower_sel = lower_part[:, None, None, None, :]
    zero_bf = jnp.zeros((), jnp.bfloat16)
    low_side = jnp.where(lower_sel, spec_rows, zero_bf)
    high_side = jnp.where(lower_sel, zero_bf, spec_rows)
    masked = jnp.stack([low_side, high_side], axis=4).reshape(pair_dev, stacked_rows, packed)
    inverse_out = lax.dot_general(
        masked, legendre, (((2,), (2,)), ((0,), (0,))), preferred_element_type=jnp.float32
    )
    inverse_out = inverse_out.reshape(pair_dev, 2, FIELDS, lev_dev, 2, cycle_count)
    legendre_out = jnp.transpose(inverse_out, (2, 3, 5, 1, 0, 4))
    my_waves = jnp.stack([my_low, TRUNC - my_low], axis=1)
    live_mask = 2 * my_waves[None, :, :] < cycle_len[:, None, None]
    legendre_out = jnp.where(live_mask[None, None, :, None, :, :], legendre_out, 0.0).astype(
        jnp.bfloat16
    )
    outgoing = legendre_out.reshape(FIELDS, lev_dev, cycle_count, 1, 4 * pair_dev)
    incoming = lax.all_to_all(outgoing, "band", split_axis=2, concat_axis=3, tiled=True)
    incoming = incoming.reshape(FIELDS, lev_dev, device_cycle_index, band_count, 2, 2 * pair_dev)
    four_re = incoming[:, :, :, :, 0, :].reshape(FIELDS, lev_dev, device_cycle_index, waves_total)
    four_im = incoming[:, :, :, :, 1, :].reshape(FIELDS, lev_dev, device_cycle_index, waves_total)
    every_wave_list = jnp.stack([pair_wave, TRUNC - pair_wave], axis=1).reshape(-1)
    my_len = lax.dynamic_slice_in_dim(cycle_len, band_id * device_cycle_index, device_cycle_index)
    my_weight = lax.dynamic_slice_in_dim(
        quad_weight, band_id * device_cycle_index, device_cycle_index
    )
    lengths = my_len[:, None, None]
    outer_num = (
        every_wave_list[None, :] * (jnp.arange(lev_count, dtype=jnp.int32) * points_dev)[:, None]
    )
    outer_cos, outer_sin = phases(outer_num[None], lengths)
    inner_num = every_wave_list[:, None] * jnp.arange(points_dev, dtype=jnp.int32)[None, :]
    inner_cos, inner_sin = phases(inner_num[None], lengths)
    inner_table = jnp.concatenate([inner_cos, inner_sin], axis=1).astype(jnp.bfloat16)
    gauss_weight = jnp.where(every_wave_list == 0, 1.0, 2.0).astype(jnp.float32)
    part_re = four_re.astype(jnp.float32)[:, :, :, None, :]
    part_im = four_im.astype(jnp.float32)[:, :, :, None, :]
    twist_re = (gauss_weight * (part_re * outer_cos - part_im * outer_sin)).astype(jnp.bfloat16)
    twist_im = (gauss_weight * (part_re * outer_sin + part_im * outer_cos)).astype(jnp.bfloat16)
    stacked = jnp.concatenate([twist_re, -twist_im], axis=-1)
    grid_vals = jnp.einsum(
        "flrak,rkb->flrab", stacked, inner_table, preferred_element_type=jnp.float32
    )
    points = (
        jnp.arange(lev_count, dtype=jnp.int32)[:, None] * points_dev
        + jnp.arange(points_dev, dtype=jnp.int32)[None, :]
    )
    inside = points[None, :, :] < lengths
    grid_vals = jnp.where(inside[None, None], grid_vals, 0.0)
    columns = lax.all_to_all(grid_vals, "lev", split_axis=3, concat_axis=1, tiled=True)
    columns = columns.reshape(FIELDS, levels, device_cycle_index, points_dev)
    level_product = (columns[0] * columns[1]).astype(jnp.bfloat16)
    mixing_tendency = jnp.einsum(
        "zet,tui->zeui", mixing, level_product, preferred_element_type=jnp.float32
    )
    summed = columns + forcing.astype(jnp.float32) + mixing_tendency
    global_pts = lev_id * points_dev + jnp.arange(points_dev, dtype=jnp.int32)
    summed = jnp.where((global_pts[None, :] < my_len[:, None])[None, None], summed, 0.0)
    summed16 = summed.astype(jnp.bfloat16).reshape(
        FIELDS, levels, device_cycle_index, 1, points_dev
    )
    cycle_q = lax.all_to_all(summed16, "lev", split_axis=1, concat_axis=3, tiled=True)
    analysed = jnp.einsum(
        "flrab,rkb->flrak", cycle_q, inner_table, preferred_element_type=jnp.float32
    )
    cos_part = analysed[..., :waves_total]
    sin_part = analysed[..., waves_total:]
    factor = (my_weight / my_len.astype(jnp.float32))[:, None]
    coeff_re = jnp.sum(cos_part * outer_cos - sin_part * outer_sin, axis=3) * factor
    coeff_im = -jnp.sum(cos_part * outer_sin + sin_part * outer_cos, axis=3) * factor
    keep_mask = 2 * every_wave_list[None, :] < my_len[:, None]
    coeff_re = jnp.where(keep_mask, coeff_re, 0.0).astype(jnp.bfloat16)
    coeff_im = jnp.where(keep_mask, coeff_im, 0.0).astype(jnp.bfloat16)
    split_shape = (FIELDS, lev_dev, device_cycle_index, band_count, 2 * pair_dev)
    stacked_out = jnp.stack([coeff_re.reshape(split_shape), coeff_im.reshape(split_shape)], axis=4)
    stacked_out = stacked_out.reshape(FIELDS, lev_dev, device_cycle_index, band_count, 4 * pair_dev)
    arrived = lax.all_to_all(stacked_out, "band", split_axis=3, concat_axis=2, tiled=True)
    arrived = arrived.reshape(FIELDS, lev_dev, cycle_count, 2, pair_dev, 2)
    arrived_rows = jnp.transpose(arrived, (4, 3, 0, 1, 5, 2)).reshape(
        pair_dev, stacked_rows, cycle_count
    )
    direct_sum = lax.dot_general(
        arrived_rows, legendre, (((2,), (1,)), ((0,), (0,))), preferred_element_type=jnp.float32
    )
    direct_sum = direct_sum.reshape(pair_dev, 2, FIELDS, lev_dev, 2, packed)
    chosen = jnp.where(lower_sel, direct_sum[:, :, :, :, 0, :], direct_sum[:, :, :, :, 1, :])
    return jnp.transpose(chosen, (1, 2, 3, 0, 4)).astype(jnp.bfloat16)


def solution(mesh):
    return jax.shard_map(
        on_device,
        mesh=mesh,
        in_specs=(
            P(None, None, "lev", "band", None),
            P("band", None, None),
            P(),
            P(),
            P(),
            P(None, None, "band", "lev"),
            P(),
        ),
        out_specs=P(None, None, "lev", "band", None),
        check_vma=False,
    )
```

profile of v0, /device:TPU:0, one launch (start us, length us, event | category | flops | bytes accessed | tf_op | source)
XLA Modules:
  0.0 520.4 jit_solution(240825080551420880)
XLA Ops:
  0.0 0.9 broadcast_subtract_fusion.1
  1.3 4.5 fusion.11
  5.8 2.4 fusion.13
  8.3 3.7 pad_maximum_fusion
  12.0 24.7 %copy.84 = bf16[160,2,2,1,2,2561]{5,4,2,1,0,3:T(2,128)(2,1)} copy(bf16[160,2,2,1,2,2561]{5,0,2,1,4,3:T(8,128)(2,1)S(1)} %pad_maximum_fusion) | data formatting | bytes 13112320 | tf_op jit(solution)/shard_map/stack | solution.py:41
  36.7 14.5 %reshape.501 = bf16[160,8,2561]{2,1,0:T(8,128)(2,1)} reshape(bf16[160,2,2,1,2,2561]{5,4,2,1,0,3:T(2,128)(2,1)} %copy.84) | data formatting | bytes 13112320 | tf_op jit(solution)/shard_map/reshape | solution.py:41
  51.5 8.8 %fusion.43 = bf16[160,8,8]{2,1,0:T(8,128)(2,1)S(1)} fusion(bf16[160,8,2561]{2,1,0:T(8,128)(2,1)} %reshape.501, bf16[160,8,2561]{2,1,0:T(8,128)(2,1)} %param.8), kind=kOutput, calls=%fused_computation.83 | convolution fusion | flops 52449280 | bytes 13132800 | tf_op jit(solution)/shard_map/dot_general | solution.py:42
  60.4 0.4 fusion.20
  60.8 0.8 copy.86
  61.5 5.2 all-to-all-start
  66.8 0.7 dynamic_slice.10
  70.0 350.4 %cosine_convert_fusion = (bf16[2560,2564]{0,1:T(8,128)(2,1)}, bf16[2560,2564]{0,1:T(8,128)(2,1)}) fusion(f32[]{:T(128)} %bitcast.4, s32[]{:T(128)} %bitcast.2, s32[2560]{0:T(1024)S(1)} %broadcast_in_dim_reshape.2, pred[]{:T(512)} %bitcast.3), kind=kLoop, calls=%fused_computation.5 | loop fusion | flops 78766080 | bytes 26265608 | tf_op jit(solution)/shard_map/convert.2
  420.4 1.2 fusion.38
  421.6 0.7 add_compare_fusion
  422.9 12.5 %fusion.19 = f32[2,1,1,4,2564]{4,3,0,1,2:T(4,128)S(1)} fusion(bf16[2560,2564]{0,1:T(8,128)(2,1)} %get-tuple-element.16, bf16[2560,2564]{0,1:T(8,128)(2,1)} %get-tuple-element.15, bf16[2,1,1,4,2560]{4,3,0,2,1:T(4,128)(2,1)S(1)} %fusion.26, bf16[2,1,1,4,2560]{4,3,0,2,1:T(4,128)(2,1)S(1)} %multiply_convert_fusion.1, pred[4,2564]{1,0:T(4,128)(4,1)S(1)} %add_compare_fusion), kind=kOutput, calls=%fused_computation.30 | convolution fusion | flops 262737952 | bytes 26429584 | tf_op jit(solution)/shard_map/flrak,rkb->flrab/dot_general | solution.py:76
  435.4 0.7 copy.88
  436.1 4.9 all-to-all-start.1
  440.9 0.6 add_compare_fusion.1
  441.6 5.2 all-to-all-done.1
  447.0 0.7 copy.91
  447.7 3.5 all-to-all-start.2
  451.2 0.7 multiply_compare_fusion
  452.5 0.7 dynamic_slice.11
  453.1 0.3 copy.78
  453.5 0.4 lt.123
  454.5 2.1 all-to-all-done.2
  456.6 11.4 %fusion.10 = f32[2,1,1,4,5120]{4,3,0,2,1:T(4,128)S(1)} fusion(bf16[2560,2564]{0,1:T(8,128)(2,1)} %get-tuple-element.16, bf16[2560,2564]{0,1:T(8,128)(2,1)} %get-tuple-element.15, bf16[2,4,1,1,2564]{4,0,3,2,1:T(2,128)(2,1)S(1)} %all-to-all-done.2), kind=kOutput, calls=%fused_computation.19 | convolution fusion | flops 262553600 | bytes 26460224 | tf_op jit(solution)/shard_map/flrab,rkb->flrak/dot_general | solution.py:98
  468.5 8.7 %all_to_all.16 = bf16[2,1,1,8,640]{4,0,2,1,3:T(2,128)(2,1)S(1)} all-to-all(bf16[2,1,1,8,640]{4,0,2,1,3:T(2,128)(2,1)S(1)} %reshape.519), channel_id=1, replica_groups=mesh['band'=8,'lev'=4] {'band'}, dimensions={3} | all-to-all | bytes 40960 | tf_op jit(solution)/shard_map/all_to_all | solution.py:112
  477.7 7.9 %fusion.44 = bf16[160,8,2561]{2,1,0:T(8,128)(2,1)} fusion(bf16[160,8,8]{2,1,0:T(8,128)(2,1)S(1)} %bitcast.113, bf16[160,8,2561]{2,1,0:T(8,128)(2,1)} %param.8), kind=kOutput, calls=%fused_computation.84 | convolution fusion | flops 52449280 | bytes 13132800 | tf_op jit(solution)/shard_map/dot_general | solution.py:117
  485.6 14.1 %reshape.512 = bf16[160,2,2,1,2,2561]{5,4,2,1,0,3:T(2,128)(2,1)} reshape(bf16[160,8,2561]{2,1,0:T(8,128)(2,1)} %fusion.44) | data formatting | bytes 13112320 | tf_op jit(solution)/shard_map/reshape | solution.py:120
  499.7 14.7 %fusion.41 = (bf16[160,2,2,1,1,2561]{5,4,2,1,0,3:T(2,128)(2,1)S(1)}, bf16[160,2,2,1,1,2561]{5,4,2,1,0,3:T(2,128)(2,1)}) fusion(bf16[160,2,2,1,2,2561]{5,4,2,1,0,3:T(2,128)(2,1)} %reshape.512), kind=kLoop, calls=%fused_computation.81 | loop fusion | bytes 13112320 | tf_op jit(solution)/shard_map/slice | solution.py:121
  514.4 6.0 %fusion.12 = bf16[2,2,1,160,2561]{4,3,2,1,0:T(8,128)(2,1)} fusion(bf16[160,2,2,1,1,2561]{5,4,2,1,0,3:T(2,128)(2,1)} %get-tuple-element.10, bf16[160,2,2,1,1,2561]{5,4,2,1,0,3:T(2,128)(2,1)S(1)} %get-tuple-element.9, pred[160,2561]{1,0:T(8,128)(4,1)S(1)} %copy-done.4), kind=kLoop, calls=%fused_computation.21 | loop fusion | flops 1639040 | bytes 10244000 | tf_op jit(solution)/shard_map/convert_element_type | solution.py:122
  (52 shorter events, 3.0 us)
Async XLA Ops:
  0.0 446.8 %copy-start = (bf16[2,4,4]{2,1,0:T(4,128)(2,1)S(1)}, bf16[2,4,4]{2,1,0:T(4,128)(2,1)}, u32[]{:S(2)}) copy-start(bf16[2,4,4]{2,1,0:T(4,128)(2,1)} %param.13) | copy-start | bytes 196
  0.0 5.8 %copy-start.2 = (bf16[2,2,1,160,2561]{4,3,2,1,0:T(8,128)(2,1)S(1)}, bf16[2,2,1,160,2561]{4,3,2,1,0:T(8,128)(2,1)}, u32[]{:S(2)}) copy-start(bf16[2,2,1,160,2561]{4,3,2,1,0:T(8,128)(2,1)} %param.7) | copy-start | bytes 9834244
  1.2 6.9 %copy-start.3 = (pred[160,2561]{1,0:T(8,128)(4,1)}, pred[160,2561]{1,0:T(8,128)(4,1)S(1)}, u32[]{:S(2)}) copy-start(pred[160,2561]{1,0:T(8,128)(4,1)S(1)} %iota_compare_fusion) | copy-start | bytes 1229284
  36.7 14.6 %copy-start.6 = (s32[8]{0:T(128)S(1)}, s32[8]{0:T(128)}, u32[]{:S(2)}) copy-start(s32[8]{0:T(128)} %param.9) | copy-start | bytes 100
  51.5 15.2 %copy-start.5 = (s32[1280]{0:T(1024)S(1)}, s32[1280]{0:T(1024)}, u32[]{:S(2)}) copy-start(s32[1280]{0:T(1024)} %param.10) | copy-start | bytes 15364
  61.5 360.8 %all-to-all-start = ((bf16[2,1,8,1,640]{4,0,3,1,2:T(2,128)(2,1)}), bf16[2,1,8,1,640]{4,0,3,1,2:T(2,128)(2,1)S(1)}, u32[]{:S(2)}, u32[]{:S(2)}) async-start(bf16[2,1,8,1,640]{4,0,3,1,2:T(2,128)(2,1)} %copy.86), calls=%async_computation | async-start | bytes 40960 | tf_op jit(solution)/shard_map/all_to_all | solution.py:53
  422.9 23.9 %copy-start.7 = (bf16[2,4,1,2564]{3,1,2,0:T(4,128)(2,1)S(1)}, bf16[2,4,1,2564]{3,1,2,0:T(4,128)(2,1)}, u32[]{:S(2)}) copy-start(bf16[2,4,1,2564]{3,1,2,0:T(4,128)(2,1)} %param.12) | copy-start | bytes 123076
  422.9 29.5 %copy-start.8 = (f32[8]{0:T(128)S(1)}, f32[8]{0:T(128)}, u32[]{:S(2)}) copy-start(f32[8]{0:T(128)} %param.11) | copy-start | bytes 100
  436.1 10.7 %all-to-all-start.1 = ((f32[2,1,1,4,2564]{4,0,1,2,3:T(2,128)}), f32[2,1,1,4,2564]{4,0,1,2,3:T(2,128)S(1)}, u32[]{:S(2)}, u32[]{:S(2)}) async-start(f32[2,1,1,4,2564]{4,0,1,2,3:T(2,128)} %copy.88), calls=%async_computation.1 | async-start | bytes 172032 | tf_op jit(solution)/shard_map/all_to_all | solution.py:85
  447.7 8.9 %all-to-all-start.2 = ((bf16[2,4,1,1,2564]{4,0,3,2,1:T(2,128)(2,1)}), bf16[2,4,1,1,2564]{4,0,3,2,1:T(2,128)(2,1)S(1)}, u32[]{:S(2)}, u32[]{:S(2)}) async-start(bf16[2,4,1,1,2564]{4,0,3,2,1:T(2,128)(2,1)} %copy.91), calls=%async_computation.2 | async-start | bytes 86016 | tf_op jit(solution)/shard_map/all_to_all | solution.py:97
  499.7 14.7 %copy-start.4 = (pred[160,2561]{1,0:T(8,128)(4,1)S(1)}, pred[160,2561]{1,0:T(8,128)(4,1)}, u32[]{:S(2)}) copy-start(pred[160,2561]{1,0:T(8,128)(4,1)} %copy-done.3) | copy-start | bytes 1229284
  514.4 6.0 %copy-start.1 = (bf16[2,4,4]{2,1,0:T(4,128)(2,1)S(1)}, bf16[2,4,4]{2,1,0:T(4,128)(2,1)}, u32[]{:S(2)}) copy-start(bf16[2,4,4]{2,1,0:T(4,128)(2,1)} %param.13) | copy-start | bytes 196
where the time goes:
time: 522 us; the launch traced here: 520 us
  other arithmetic  373 us (71%)
  local copies, waits for them, and re-layouts  73.9 us (14%)
  matrix products  40.8 us (8%)
  starting transfers between devices  13.6 us (3%)
  blocking collectives  8.74 us (2%)
  waiting for transfers between devices  7.25 us (1%)
    another operation x1, other arithmetic  350 us
    another operation x1, local copies, waits for them, and re-layouts, on_device(): jnp.stack([low_side, high_side], axis=4)  24.7 us
    slice x1, local copies, waits for them, and re-layouts, on_device(): direct_sum[:, :, :, :, 0, :]  14.7 us
    reshape x1, local copies, waits for them, and re-layouts, on_device(): jnp.stack([low_side, high_side], axis=4)  14.5 us
    reshape x1, local copies, waits for them, and re-layouts, on_device(): direct_sum = direct_sum.reshape(pair_dev, 2, FIELDS, lev_dev, 2, packed)  14.1 us
    dot_general x1, matrix products, on_device(): jnp.einsum('flrak,rkb->flrab', stacked, inner_table, preferred_element_ty...  12.5 us
    dot_general x1, matrix products, on_device(): jnp.einsum('flrab,rkb->flrak', cycle_q, inner_table, preferred_element_ty...  11.4 us
    another operation x3, other arithmetic, on_device(): jnp.stack([low_side, high_side], axis=4)  10.6 us
  transfers between devices with their start and end apart: 3, of which 2 were waited for; matrix products, arithmetic and copies ran while one was open for 68% of the time, Pallas kernels for 0%

commit v1 on v0

v1 whole, which is shorter than its diff:
```python
import functools

import jax
import jax.numpy as jnp
from jax import lax
from jax.experimental import pallas as pl
from jax.experimental.pallas import tpu as pltpu
from jax.sharding import PartitionSpec as P

TRUNC = 2559
FIELDS = 2
INNER = 256
CHUNK = 256
TWO_PI = 6.283185307179586


def pair_block(pair_dev):
    return 16 if pair_dev % 16 == 0 else 8


def sincos(wave, point, length, inverse_length):
    number = wave * point
    turns = jnp.floor(number.astype(jnp.float32) * inverse_length).astype(jnp.int32)
    residue = (number - turns * length).astype(jnp.float32) * inverse_length
    quarter = jnp.floor(residue * 4.0 + 0.5)
    t = (residue - quarter * 0.25) * TWO_PI
    t2 = t * t
    sin_t = t * (1.0 + t2 * (-1.0 / 6 + t2 * (1.0 / 120 + t2 * (-1.0 / 5040 + t2 * (1.0 / 362880)))))
    cos_t = 1.0 + t2 * (
        -0.5 + t2 * (1.0 / 24 + t2 * (-1.0 / 720 + t2 * (1.0 / 40320 + t2 * (-1.0 / 3628800))))
    )
    q = quarter.astype(jnp.int32)
    swap = (q & 1) == 1
    cos_v = jnp.where(swap, sin_t, cos_t)
    sin_v = jnp.where(swap, cos_t, sin_t)
    cos_v = jnp.where(((q + 1) & 2) == 2, -cos_v, cos_v)
    sin_v = jnp.where((q & 2) == 2, -sin_v, sin_v)
    return cos_v, sin_v


def diagonal(pairs, cycles):
    rows = lax.broadcasted_iota(jnp.int32, (pairs, cycles, 8 * pairs), 0)
    lanes = lax.broadcasted_iota(jnp.int32, (pairs, cycles, 8 * pairs), 2) % pairs
    return rows == lanes


def inverse_kernel(limit_ref, spec_ref, leg_ref, out_ref):
    pairs, cycles, packed = leg_ref.shape
    column = lax.broadcasted_iota(jnp.int32, (pairs, packed), 1)
    lower = column < limit_ref[...]
    lows, highs = [], []
    for s in range(2):
        for f in range(FIELDS):
            row = spec_ref[s, f, 0].astype(jnp.float32)
            lows.append(jnp.where(lower, row, 0.0))
            highs.append(jnp.where(lower, 0.0, row))
    spec = jnp.concatenate(lows + highs, axis=0).astype(jnp.bfloat16)
    leg = leg_ref[...].reshape(pairs * cycles, packed)
    full = lax.dot_general(
        leg, spec, (((1,), (1,)), ((), ())), preferred_element_type=jnp.float32
    )
    full = full.reshape(pairs, cycles, 8 * pairs)
    out_ref[0] = jnp.sum(jnp.where(diagonal(pairs, cycles), full, 0.0), axis=0)


def direct_kernel(limit_ref, coeff_ref, leg_ref, out_ref):
    pairs, cycles, packed = leg_ref.shape
    wide = jnp.broadcast_to(coeff_ref[...], (pairs, cycles, 8 * pairs))
    wide = jnp.where(diagonal(pairs, cycles), wide, 0.0).reshape(pairs * cycles, 8 * pairs)
    wide = wide.T.astype(jnp.bfloat16)
    leg = leg_ref[...].reshape(pairs * cycles, packed)
    full = jnp.dot(wide, leg, preferred_element_type=jnp.float32)
    column = lax.broadcasted_iota(jnp.int32, (pairs, packed), 1)
    lower = column < limit_ref[...]
    for s in range(2):
        for f in range(FIELDS):
            at = (s * FIELDS + f) * pairs
            low = full[at : at + pairs]
            high = full[4 * pairs + at : 4 * pairs + at + pairs]
            out_ref[s, f, 0] = jnp.where(lower, low, high).astype(jnp.bfloat16)


def grid_kernel(
    points_dev, scalars_ref, factors_ref, wave_ref, four_ref, forcing_ref, mixing_ref, out_ref,
    cos_tab, sin_tab, cos_out, sin_out, twist_re, twist_im,
):
    rows, waves = four_ref.shape[1], four_ref.shape[2]
    levels = rows // FIELDS
    outer = cos_out.shape[0]
    used = pl.cdiv(points_dev, INNER)
    length = scalars_ref[0]
    base = scalars_ref[1]
    inverse_length = factors_ref[0]
    factor = factors_ref[1]

    @pl.loop(0, waves // CHUNK)
    def _(c):
        span = pl.ds(pl.multiple_of(c * CHUNK, CHUNK), CHUNK)
        wave = wave_ref[:, span]
        eight = lax.broadcasted_iota(jnp.int32, (8, CHUNK), 0)
        c0, s0 = sincos(wave, eight, length, inverse_length)
        c1, s1 = sincos(wave, eight * 8, length, inverse_length)
        c2, s2 = sincos(wave, eight * 64, length, inverse_length)
        steps = lax.broadcasted_iota(jnp.int32, (outer, CHUNK), 0)
        c3, s3 = sincos(wave, base + steps * INNER, length, inverse_length)
        cos_out[:, span] = c3
        sin_out[:, span] = s3
        for high in range(INNER // 64):
            ch, sh = c2[high : high + 1], s2[high : high + 1]
            for mid in range(8):
                cm, sm = c1[mid : mid + 1], s1[mid : mid + 1]
                cj, sj = ch * cm - sh * sm, ch * sm + sh * cm
                at = high * 64 + mid * 8
                cos_tab[at : at + 8, span] = (c0 * cj - s0 * sj).astype(jnp.bfloat16)
                sin_tab[at : at + 8, span] = (s0 * cj + c0 * sj).astype(jnp.bfloat16)

    @pl.loop(0, waves // CHUNK)
    def _(c):
        span = pl.ds(pl.multiple_of(c * CHUNK, CHUNK), CHUNK)
        wave = wave_ref[:, span]
        gain = jnp.where(wave == 0, 1.0, 2.0)
        gain = jnp.where(2 * wave < length, gain, 0.0)
        live = gain > 0.0
        re = jnp.where(live, four_ref[0, :, span].astype(jnp.float32) * gain, 0.0)
        im = jnp.where(live, four_ref[1, :, span].astype(jnp.float32) * gain, 0.0)
        for a in range(used):
            co, so = cos_out[a : a + 1, span], sin_out[a : a + 1, span]
            twist_re[a * rows : (a + 1) * rows, span] = (re * co - im * so).astype(jnp.bfloat16)
            twist_im[a * rows : (a + 1) * rows, span] = -(re * so + im * co).astype(jnp.bfloat16)

    contract = (((1,), (1,)), ((), ()))
    grid = lax.dot_general(
        twist_re[...], cos_tab[...], contract, preferred_element_type=jnp.float32
    ) + lax.dot_general(twist_im[...], sin_tab[...], contract, preferred_element_type=jnp.float32)
    lane = lax.broadcasted_iota(jnp.int32, (rows, INNER), 1)
    updated = []
    for a in range(used):
        point = a * INNER + lane
        inside = (point < points_dev) & (base + point < length)
        cell = jnp.where(inside, grid[a * rows : (a + 1) * rows], 0.0)
        product = (cell[:levels] * cell[levels:]).astype(jnp.bfloat16).astype(jnp.float32)
        total = cell + forcing_ref[:, a * INNER : (a + 1) * INNER].astype(jnp.float32)
        for l2 in range(levels):
            total = total + mixing_ref[:, l2 : l2 + 1] * product[l2 : l2 + 1]
        updated.append(jnp.where(inside, total, 0.0))
    updated = jnp.concatenate(updated, axis=0).astype(jnp.bfloat16)

    @pl.loop(0, waves // CHUNK)
    def _(c):
        span = pl.ds(pl.multiple_of(c * CHUNK, CHUNK), CHUNK)
        cos_part = jnp.dot(updated, cos_tab[:, span], preferred_element_type=jnp.float32)
        sin_part = jnp.dot(updated, sin_tab[:, span], preferred_element_type=jnp.float32)
        re = jnp.zeros((rows, CHUNK), jnp.float32)
        im = jnp.zeros((rows, CHUNK), jnp.float32)
        for a in range(used):
            co, so = cos_out[a : a + 1, span], sin_out[a : a + 1, span]
            cp, sp = cos_part[a * rows : (a + 1) * rows], sin_part[a * rows : (a + 1) * rows]
            re = re + (cp * co - sp * so)
            im = im + (cp * so + sp * co)
        keep = 2 * wave_ref[:, span] < length
        out_ref[0, :, span] = jnp.where(keep, re * factor, 0.0).astype(jnp.bfloat16)
        out_ref[1, :, span] = jnp.where(keep, im * -factor, 0.0).astype(jnp.bfloat16)


def on_device(spectral, legendre, cycle_len, pair_wave, quad_weight, forcing, mixing):
    band_count = lax.axis_size("band")
    lev_count = lax.axis_size("lev")
    band_id = lax.axis_index("band")
    lev_id = lax.axis_index("lev")
    pair_dev, packed = spectral.shape[3], spectral.shape[4]
    cycles = legendre.shape[1]
    levels, points_dev = forcing.shape[1], forcing.shape[3]
    rows = FIELDS * levels
    waves = 2 * band_count * pair_dev
    pairs = pair_block(pair_dev)
    blocks = pair_dev // pairs

    my_low = lax.dynamic_slice_in_dim(pair_wave, band_id * pair_dev, pair_dev)
    limit = (TRUNC + 1 - my_low)[:, None]
    spec_spec = pl.BlockSpec((2, FIELDS, 1, pairs, packed), lambda i: (0, 0, 0, i, 0))
    leg_spec = pl.BlockSpec((pairs, cycles, packed), lambda i: (i, 0, 0))
    limit_spec = pl.BlockSpec((pairs, 1), lambda i: (i, 0))
    cell_spec = pl.BlockSpec((1, cycles, 8 * pairs), lambda i: (i, 0, 0))
    four = pl.pallas_call(
        inverse_kernel,
        grid=(blocks,),
        in_specs=[limit_spec, spec_spec, leg_spec],
        out_specs=cell_spec,
        out_shape=jax.ShapeDtypeStruct((blocks, cycles, 8 * pairs), jnp.float32),
    )(limit, spectral, legendre)
    four = four.astype(jnp.bfloat16).reshape(blocks, cycles, 2, 4, pairs)
    four = jnp.transpose(four, (1, 3, 0, 2, 4)).reshape(cycles, 1, 4 * blocks * 2 * pairs)
    four = jnp.broadcast_to(four, (cycles, lev_count, four.shape[2]))
    four = four.reshape(band_count * lev_count, four.shape[2])
    four = lax.all_to_all(four, ("band", "lev"), split_axis=0, concat_axis=0, tiled=True)
    four = four.reshape(band_count, lev_count, 2, FIELDS, 2 * pair_dev)
    four = jnp.transpose(four, (2, 3, 1, 0, 4)).reshape(2, rows, waves)

    low = pair_wave.reshape(band_count, blocks, 1, pairs)
    wave = jnp.concatenate([low, TRUNC - low], axis=2).reshape(1, waves)
    my_len = lax.dynamic_index_in_dim(cycle_len, band_id, 0, keepdims=False)
    my_weight = lax.dynamic_index_in_dim(quad_weight, band_id, 0, keepdims=False)
    length_f = my_len.astype(jnp.float32)
    scalars = jnp.stack([my_len, lev_id * points_dev])
    factors = jnp.stack([1.0 / length_f, my_weight / length_f])
    used = pl.cdiv(points_dev, INNER)
    outer = pl.cdiv(used, 8) * 8
    force = jnp.pad(forcing.reshape(rows, points_dev), ((0, 0), (0, used * INNER - points_dev)))
    vmem = pl.BlockSpec(memory_space=pltpu.VMEM)
    smem = pl.BlockSpec(memory_space=pltpu.SMEM)
    partial = pl.pallas_call(
        functools.partial(grid_kernel, points_dev),
        in_specs=[smem, smem, vmem, vmem, vmem, vmem],
        out_specs=vmem,
        out_shape=jax.ShapeDtypeStruct((2, rows, waves), jnp.bfloat16),
        scratch_shapes=[
            pltpu.VMEM((INNER, waves), jnp.bfloat16),
            pltpu.VMEM((INNER, waves), jnp.bfloat16),
            pltpu.VMEM((outer, waves), jnp.float32),
            pltpu.VMEM((outer, waves), jnp.float32),
            pltpu.VMEM((used * rows, waves), jnp.bfloat16),
            pltpu.VMEM((used * rows, waves), jnp.bfloat16),
        ],
    )(scalars, factors, wave, four, force, mixing.reshape(rows, levels).astype(jnp.float32))

    back = partial.reshape(2, FIELDS, lev_count, band_count, 2 * pair_dev)
    back = jnp.transpose(back, (3, 2, 0, 1, 4)).reshape(band_count * lev_count, 8 * pair_dev)
    back = lax.all_to_all(back, ("band", "lev"), split_axis=0, concat_axis=0, tiled=True)
    back = back.reshape(band_count, lev_count, 4, blocks, 2, pairs).astype(jnp.float32)
    back = jnp.sum(back, axis=1)
    coeff = jnp.transpose(back, (2, 0, 3, 1, 4)).reshape(blocks, cycles, 8 * pairs)
    return pl.pallas_call(
        direct_kernel,
        grid=(blocks,),
        in_specs=[limit_spec, cell_spec, leg_spec],
        out_specs=spec_spec,
        out_shape=jax.ShapeDtypeStruct(spectral.shape, jnp.bfloat16),
    )(limit, coeff, legendre)


def solution(mesh):
    return jax.shard_map(
        on_device,
        mesh=mesh,
        in_specs=(
            P(None, None, "lev", "band", None),
            P("band", None, None),
            P(),
            P(),
            P(),
            P(None, None, "band", "lev"),
            P(),
        ),
        out_specs=P(None, None, "lev", "band", None),
        check_vma=False,
    )
```

time: 522 us -> 66.9 us (0.13)
  other arithmetic: 373 us -> 8.05 us
  local copies, waits for them, and re-layouts: 73.9 us -> 10.1 us
  matrix products: 40.8 us -> 0 us
  Pallas kernels: 0 us -> 25.8 us
  starting transfers between devices: 13.6 us -> 7.32 us
  waiting for transfers between devices: 7.25 us -> 1.17 us
    another operation x6 -> x2, other arithmetic: 361 us -> 1.81 us  [the longest x1 1.2 us: on_device(): scalars = jnp.stack([my_len, lev_id * points_dev])]
    dot_general x5 -> x0, matrix products: 40.8 us -> none  [the longest x1 12.5 us: on_device(): jnp.einsum('flrak,rkb->flrab', stacked, inner_table, preferred_element_ty...]
    reshape x7 -> x10, local copies, waits for them, and re-layouts: 30.2 us -> 3.98 us  [the longest x2 1.09 us: on_device(): back = partial.reshape(2, FIELDS, lev_count, band_count, 2 * pair_dev)]
    pallas_call x0 -> x3, Pallas kernels: none -> 25.8 us  [the longest x1 9.8 us: on_device(): pl.pallas_call(inverse_kernel, grid=(blocks,), in_specs=[limit_spec, spec...]
    another operation x5 -> x0, local copies, waits for them, and re-layouts: 25.3 us -> none  [the longest x1 24.7 us: on_device(): jnp.stack([low_side, high_side], axis=4)]
    slice x2 -> x0, local copies, waits for them, and re-layouts: 14.7 us -> none  [the longest x1 14.7 us: on_device(): direct_sum[:, :, :, :, 0, :]]
    all_to_all x3 -> x1, starting transfers between devices: 13.6 us -> 7.32 us  [on_device(): lax.all_to_all(four, ('band', 'lev'), split_axis=0, concat_axis=0, tiled=...]
    all_to_all x3 -> x1, waiting for transfers between devices: 7.25 us -> 1.17 us  [on_device(): lax.all_to_all(four, ('band', 'lev'), split_axis=0, concat_axis=0, tiled=...]
  transfers between devices with their start and end apart: 3 -> 1, of which waited for: 2 -> 1; matrix products, arithmetic and copies ran while one was open for 68% -> 8% of each run, Pallas kernels for 0% -> 0%
where the time goes in v1:
time: 66.9 us; the launch traced here: 66.1 us
  Pallas kernels  25.8 us (39%)
  blocking collectives  12.2 us (18%)
  local copies, waits for them, and re-layouts  10.1 us (15%)
  other arithmetic  8.05 us (12%)
  starting transfers between devices  7.32 us (11%)
  between operations  1.45 us (2%)
  waiting for transfers between devices  1.17 us (2%)
    all_to_all x1, blocking collectives, on_device(): lax.all_to_all(back, ('band', 'lev'), split_axis=0, concat_axis=0, tiled=...  12.2 us
    pallas_call x1, Pallas kernels, on_device(): pl.pallas_call(inverse_kernel, grid=(blocks,), in_specs=[limit_spec, spec...  9.8 us
    pallas_call x1, Pallas kernels, on_device(): pl.pallas_call(direct_kernel, grid=(blocks,), in_specs=[limit_spec, cell_...  9.61 us
    all_to_all x1, starting transfers between devices, on_device(): lax.all_to_all(four, ('band', 'lev'), split_axis=0, concat_axis=0, tiled=...  7.32 us
    pallas_call x1, Pallas kernels, on_device(): pl.pallas_call(functools.partial(grid_kernel, points_dev), in_specs=[smem...  6.41 us
    convert_element_type x1, local copies, waits for them, and re-layouts, on_device(): back.reshape(band_count, lev_count, 4, blocks, 2, pairs).astype(jnp.float32)  1.72 us
    all_to_all x2, other arithmetic, on_device(): lax.all_to_all(four, ('band', 'lev'), split_axis=0, concat_axis=0, tiled=...  1.54 us
  transfers between devices with their start and end apart: 1, of which 1 were waited for; matrix products, arithmetic and copies ran while one was open for 8% of the time, Pallas kernels for 0%

profile of v1, /device:TPU:0, one launch (start us, length us, event | category | flops | bytes accessed | tf_op | source)
XLA Modules:
  0.0 66.1 jit_solution(8081511911792241035)
XLA Ops:
  0.0 0.8 %dynamic-slice_subtract_fusion = s32[160]{0:T(256)S(1)} fusion(s32[1280]{0:T(1024)} %param.10, s32[]{:T(128)S(6)} %select_n.9), kind=kLoop, calls=%fused_computation.5 | loop fusion | flops 160 | bytes 1284 | tf_op jit(solution)/shard_map/sub | solution.py:179
  0.8 0.7 %copy.35.limit_ref = s32[160,1]{1,0:T(8,128)} copy(s32[160,1]{0,1:T(1,128)S(1)} %bitcast.20) | data formatting | bytes 1280 | tf_op jit(solution)/shard_map/broadcast_in_dim | solution.py:179
  1.5 9.8 %shard_map.73 = f32[10,8,128]{2,1,0:T(8,128)} custom-call(s32[160,1]{1,0:T(8,128)} %copy.35.limit_ref, bf16[2,2,1,160,2561]{4,3,2,1,0:T(8,128)(2,1)} %spec_ref.1, bf16[160,8,2561]{2,1,0:T(8,128)(2,1)} %leg_ref.3), custom_call_target="tpu_custom_call" | custom-call | tf_op jit(solution)/shard_map/pallas_call | solution.py:184
  11.3 0.8 %convert_element_type.24 = bf16[10,8,128]{2,1,0:T(8,128)(2,1)S(1)} convert(f32[10,8,128]{2,1,0:T(8,128)} %shard_map.73) | non-fusion elementwise | flops 10240 | bytes 61440 | tf_op jit(solution)/shard_map/convert_element_type | solution.py:191
  12.1 0.1 reshape.62
  12.3 0.1 copy.39
  12.4 0.2 broadcast_in_dim.11
  12.7 0.5 broadcast.12
  13.2 1.1 %reduce.3 = bf16[32,1280]{1,0:T(8,128)(2,1)S(1)} reduce(bf16[32,1,1280]{2,1,0:T(2,128)(2,1)S(1)} %all_to_all.16, bf16[]{:T(256)} %broadcast.12), dimensions={1}, to_apply=%all_to_all.16.reduce_sub_computation | reduce | bytes 163842 | tf_op jit(solution)/shard_map/all_to_all | solution.py:195
  14.3 0.7 reshape.72
  15.0 7.3 %all-to-all-start = ((bf16[32,2,640]{2,1,0:T(2,128)(2,1)}), bf16[32,2,640]{2,1,0:T(2,128)(2,1)S(1)}, u32[]{:S(2)}, u32[]{:S(2)}) async-start(bf16[32,2,640]{2,1,0:T(2,128)(2,1)} %reshape.72), calls=%async_computation | async-start | bytes 163840 | tf_op jit(solution)/shard_map/all_to_all | solution.py:195
  22.6 0.6 dynamic_slice.12
  23.2 1.2 %pad_add_fusion.1.scalars_ref = s32[2]{0:T(128)} fusion(s32[1]{0:T(128)} %bitcast.1, s32[1]{0:T(128)} %dynamic_slice.12), kind=kLoop, calls=%fused_computation.6 | loop fusion | flops 2 | bytes 16 | tf_op jit(solution)/shard_map/stack | solution.py:204
  25.0 0.6 dynamic_slice.13
  26.2 0.6 convert.2.mixing_ref
  26.8 0.7 %reshape.61.wave_ref = s32[1,2560]{1,0:T(1,128)} reshape(s32[8,10,2,16]{3,2,1,0:T(2,128)S(1)} %pad_add_fusion) | data formatting | bytes 20480 | tf_op jit(solution)/shard_map/reshape | solution.py:200
  27.6 0.6 pad.4.forcing_ref
  28.2 0.6 pad_maximum_fusion.factors_ref
  28.8 1.2 %all-to-all-done = bf16[32,2,640]{2,1,0:T(2,128)(2,1)S(1)} async-done(((bf16[32,2,640]{2,1,0:T(2,128)(2,1)}), bf16[32,2,640]{2,1,0:T(2,128)(2,1)S(1)}, u32[]{:S(2)}, u32[]{:S(2)}) %all-to-all-start) | async-done | bytes 81952 | tf_op jit(solution)/shard_map/all_to_all | solution.py:195
  30.1 0.5 reduce
  30.5 0.1 reshape.63
  30.7 0.8 %reshape.64.four_ref = bf16[2,8,2560]{2,1,0:T(8,128)(2,1)} reshape(bf16[2,2,4,8,320]{4,3,2,1,0:T(8,128)(2,1)S(1)} %copy.29) | data formatting | bytes 163840 | tf_op jit(solution)/shard_map/reshape | solution.py:197
  31.4 6.4 %shard_map.74 = bf16[2,8,2560]{2,1,0:T(8,128)(2,1)} custom-call(s32[2]{0:T(128)} %pad_add_fusion.1.scalars_ref, f32[2]{0:T(128)} %pad_maximum_fusion.factors_ref, s32[1,2560]{1,0:T(1,128)} %reshape.61.wave_ref, bf16[2,8,2560]{2,1,0:T(8,128)(2,1)} %reshape.64.four_ref, bf16[8,2816]{1,0:T(8,128)(2,1)} %pad.4.forcing_ref, f32[8,4]{1,0:T(8,128)} %convert.2.mixing_ref), custom_call_target="tpu_custom_call" | custom-call | tf_op jit(solution)/shard_map/pallas_call | solution.py:211
  37.9 1.0 %reshape.66 = bf16[2,2,4,8,320]{4,3,2,1,0:T(8,128)(2,1)S(1)} reshape(bf16[2,8,2560]{2,1,0:T(8,128)(2,1)} %shard_map.74) | data formatting | bytes 163840 | tf_op jit(solution)/shard_map/reshape | solution.py:226
  39.0 0.2 all_to_all.17
  39.1 1.1 %reduce.4 = bf16[32,1280]{1,0:T(8,128)(2,1)S(1)} reduce(bf16[32,1,1280]{2,1,0:T(2,128)(2,1)S(1)} %all_to_all.17, bf16[]{:T(256)} %broadcast.12), dimensions={1}, to_apply=%all_to_all.17.reduce_sub_computation | reduce | bytes 163842 | tf_op jit(solution)/shard_map/all_to_all | solution.py:228
  40.2 12.2 %all_to_all.20 = bf16[32,2,640]{2,1,0:T(2,128)(2,1)S(1)} all-to-all(bf16[32,2,640]{2,1,0:T(2,128)(2,1)S(1)} %reshape.74), channel_id=1, replica_groups=mesh['band'=8,'lev'=4] {'band','lev'}, dimensions={0} | all-to-all | bytes 163840 | tf_op jit(solution)/shard_map/all_to_all | solution.py:228
  52.5 0.4 convert_reduce_fusion
  52.9 1.7 %reshape.69 = f32[8,4,4,10,2,16]{5,4,3,2,1,0:T(2,128)S(1)} reshape(f32[32,1280]{1,0:T(8,128)S(1)} %convert_reduce_fusion) | data formatting | bytes 327680 | tf_op jit(solution)/shard_map/convert_element_type | solution.py:229
  54.6 0.9 %reduce_sum.9 = f32[8,4,10,2,16]{4,3,2,1,0:T(2,128)S(1)} reduce(f32[8,4,4,10,2,16]{5,4,3,2,1,0:T(2,128)S(1)} %reshape.69, f32[]{:T(128)} %constant.36.clone.1), dimensions={1}, to_apply=%region_0.1 | reduce | flops 30720 | bytes 204804 | tf_op jit(solution)/shard_map/reduce_sum | solution.py:230
  55.7 0.8 %reshape.67.coeff_ref = f32[10,8,128]{2,1,0:T(8,128)} reshape(f32[10,8,2,4,16]{4,3,2,1,0:T(4,128)S(1)} %copy.34) | data formatting | bytes 81920 | tf_op jit(solution)/shard_map/reshape | solution.py:231
  56.5 9.6 %shard_map.75 = bf16[2,2,1,160,2561]{4,3,2,1,0:T(8,128)(2,1)} custom-call(s32[160,1]{1,0:T(8,128)} %copy.35.limit_ref, f32[10,8,128]{2,1,0:T(8,128)} %reshape.67.coeff_ref, bf16[160,8,2561]{2,1,0:T(8,128)(2,1)} %leg_ref.3), custom_call_target="tpu_custom_call" | custom-call | tf_op jit(solution)/shard_map/pallas_call | solution.py:232
  (22 shorter events, 0.7 us)
Async XLA Ops:
  1.5 20.8 %copy-start.1 = (s32[1280]{0:T(1024)S(1)}, s32[1280]{0:T(1024)}, u32[]{:S(2)}) copy-start(s32[1280]{0:T(1024)} %param.10) | copy-start | bytes 15364
  1.5 21.1 %copy-start.3 = (s32[8]{0:T(128)S(1)}, s32[8]{0:T(128)}, u32[]{:S(2)}) copy-start(s32[8]{0:T(128)} %param.9) | copy-start | bytes 100
  1.5 23.4 %copy-start.4 = (f32[8]{0:T(128)S(1)}, f32[8]{0:T(128)}, u32[]{:S(2)}) copy-start(f32[8]{0:T(128)} %param.11) | copy-start | bytes 100
  1.5 24.7 %copy-start.2 = (bf16[2,4,4]{2,1,0:T(4,128)(2,1)S(1)}, bf16[2,4,4]{2,1,0:T(4,128)(2,1)}, u32[]{:S(2)}) copy-start(bf16[2,4,4]{2,1,0:T(4,128)(2,1)} %param.13) | copy-start | bytes 196
  1.5 26.0 %copy-start = (bf16[2,4,1,2564]{3,1,2,0:T(4,128)(2,1)S(1)}, bf16[2,4,1,2564]{3,1,2,0:T(4,128)(2,1)}, u32[]{:S(2)}) copy-start(bf16[2,4,1,2564]{3,1,2,0:T(4,128)(2,1)} %param.12) | copy-start | bytes 123076
  15.0 15.0 %all-to-all-start = ((bf16[32,2,640]{2,1,0:T(2,128)(2,1)}), bf16[32,2,640]{2,1,0:T(2,128)(2,1)S(1)}, u32[]{:S(2)}, u32[]{:S(2)}) async-start(bf16[32,2,640]{2,1,0:T(2,128)(2,1)} %reshape.72), calls=%async_computation | async-start | bytes 163840 | tf_op jit(solution)/shard_map/all_to_all | solution.py:195

commit v2 on v1

v2 whole, which is shorter than its diff:
```python
import functools

import jax
import jax.numpy as jnp
from jax import lax
from jax.experimental import pallas as pl
from jax.experimental.pallas import tpu as pltpu
from jax.sharding import PartitionSpec as P

TRUNC = 2559
FIELDS = 2
INNER = 256
TWO_PI = 6.283185307179586


def pair_block(pair_dev):
    return 16 if pair_dev % 16 == 0 else 8


def sincos(wave, point, length, inverse_length):
    number = wave * point
    turns = jnp.floor(number.astype(jnp.float32) * inverse_length).astype(jnp.int32)
    residue = (number - turns * length).astype(jnp.float32) * inverse_length
    quarter = jnp.floor(residue * 4.0 + 0.5)
    t = (residue - quarter * 0.25) * TWO_PI
    t2 = t * t
    sin_t = t * (1.0 + t2 * (-1.0 / 6 + t2 * (1.0 / 120 + t2 * (-1.0 / 5040 + t2 * (1.0 / 362880)))))
    cos_t = 1.0 + t2 * (
        -0.5 + t2 * (1.0 / 24 + t2 * (-1.0 / 720 + t2 * (1.0 / 40320 + t2 * (-1.0 / 3628800))))
    )
    q = quarter.astype(jnp.int32)
    swap = (q & 1) == 1
    cos_v = jnp.where(swap, sin_t, cos_t)
    sin_v = jnp.where(swap, cos_t, sin_t)
    cos_v = jnp.where(((q + 1) & 2) == 2, -cos_v, cos_v)
    sin_v = jnp.where((q & 2) == 2, -sin_v, sin_v)
    return cos_v, sin_v


def diagonal(pairs, cycles):
    rows = lax.broadcasted_iota(jnp.int32, (pairs, cycles, 8 * pairs), 0)
    lanes = lax.broadcasted_iota(jnp.int32, (pairs, cycles, 8 * pairs), 2) % pairs
    return rows == lanes


def inverse_kernel(limit_ref, spec_ref, leg_ref, out_ref):
    pairs, cycles, packed = leg_ref.shape
    column = lax.broadcasted_iota(jnp.int32, (pairs, packed), 1)
    lower = column < limit_ref[...]
    halves = []
    for s in range(2):
        for f in range(FIELDS):
            row = spec_ref[s, f, 0].astype(jnp.float32)
            halves += [jnp.where(lower, row, 0.0), jnp.where(lower, 0.0, row)]
    spec = jnp.concatenate(halves, axis=0).astype(jnp.bfloat16)
    leg = leg_ref[...].reshape(pairs * cycles, packed)
    full = lax.dot_general(
        leg, spec, (((1,), (1,)), ((), ())), preferred_element_type=jnp.float32
    )
    full = full.reshape(pairs, cycles, 8 * pairs)
    out_ref[0] = jnp.sum(jnp.where(diagonal(pairs, cycles), full, 0.0), axis=0)


def direct_kernel(limit_ref, coeff_ref, leg_ref, out_ref):
    pairs, cycles, packed = leg_ref.shape
    wide = jnp.broadcast_to(coeff_ref[...], (pairs, cycles, 8 * pairs))
    wide = jnp.where(diagonal(pairs, cycles), wide, 0.0).reshape(pairs * cycles, 8 * pairs)
    wide = wide.T.astype(jnp.bfloat16)
    leg = leg_ref[...].reshape(pairs * cycles, packed)
    full = jnp.dot(wide, leg, preferred_element_type=jnp.float32)
    column = lax.broadcasted_iota(jnp.int32, (pairs, packed), 1)
    lower = column < limit_ref[...]
    for s in range(2):
        for f in range(FIELDS):
            at = (s * FIELDS + f) * 2 * pairs
            low = full[at : at + pairs]
            high = full[at + pairs : at + 2 * pairs]
            out_ref[s, f, 0] = jnp.where(lower, low, high).astype(jnp.bfloat16)


def grid_kernel(
    points_dev, levs, length_ref, weight_ref, wave_ref, four_ref, forcing_ref, mixing_ref, out_ref,
    cos_tab, sin_tab, cos_out, sin_out, twist_re, twist_im,
    outgoing, incoming, partial, arrived, send_sem, recv_sem, send_back, recv_back,
):
    blocks, cycles, wide = four_ref.shape
    each = wide // 4
    rows = FIELDS * levs
    outer = cos_out.shape[0]
    used = pl.cdiv(points_dev, INNER)
    slots, _, lanes = incoming.shape
    bands = slots // levs
    band_id = lax.axis_index("band")
    lev_id = lax.axis_index("lev")
    me = band_id * levs + lev_id
    length = length_ref[band_id]
    base = lev_id * points_dev
    inverse_length = 1.0 / jnp.full((1, lanes), length, jnp.int32).astype(jnp.float32)
    factor = inverse_length * weight_ref[band_id]

    barrier = pltpu.get_barrier_semaphore()

    def other(step):
        peer = (me + step) % slots
        return peer // levs, peer % levs

    @pl.loop(1, slots)
    def _(step):
        band, lev = other(step)
        pl.semaphore_signal(
            barrier, inc=1, device_id={"band": band, "lev": lev}, device_id_type=pl.DeviceIdType.MESH
        )

    sides = []
    for k in range(4):
        parts = [four_ref[i, :, k * each : (k + 1) * each] for i in range(blocks)]
        if lanes > blocks * each:
            parts.append(jnp.zeros((cycles, lanes - blocks * each), jnp.float32))
        sides.append(jnp.concatenate(parts, axis=1))
    for j in range(cycles):
        block = jnp.concatenate([side[j : j + 1] for side in sides], axis=0)
        outgoing[j] = block.astype(jnp.bfloat16)

    def tables(c):
        span = pl.ds(pl.multiple_of(c * lanes, lanes), lanes)
        wave = wave_ref[:, span]
        eight = lax.broadcasted_iota(jnp.int32, (8, lanes), 0)
        c0, s0 = sincos(wave, eight, length, inverse_length)
        c1, s1 = sincos(wave, eight * 8, length, inverse_length)
        c2, s2 = sincos(wave, eight * 64, length, inverse_length)
        steps = lax.broadcasted_iota(jnp.int32, (outer, lanes), 0)
        c3, s3 = sincos(wave, base + steps * INNER, length, inverse_length)
        cos_out[:, span] = c3
        sin_out[:, span] = s3
        for high in range(INNER // 64):
            ch, sh = c2[high : high + 1], s2[high : high + 1]
            for mid in range(8):
                cm, sm = c1[mid : mid + 1], s1[mid : mid + 1]
                cj, sj = ch * cm - sh * sm, ch * sm + sh * cm
                at = high * 64 + mid * 8
                cos_tab[at : at + 8, span] = (c0 * cj - s0 * sj).astype(jnp.bfloat16)
                sin_tab[at : at + 8, span] = (s0 * cj + c0 * sj).astype(jnp.bfloat16)

    early = bands // 2
    pl.loop(0, early)(tables)
    pl.semaphore_wait(barrier, slots - 1)

    @pl.loop(1, slots)
    def _(step):
        band, lev = other(step)
        pltpu.make_async_remote_copy(
            src_ref=outgoing.at[band], dst_ref=incoming.at[me], send_sem=send_sem,
            recv_sem=recv_sem, device_id={"band": band, "lev": lev},
            device_id_type=pl.DeviceIdType.MESH,
        ).start()

    incoming[me] = outgoing[band_id]
    pl.loop(early, bands)(tables)

    def wait_all(semaphore, buffer):
        most = buffer.at[pl.ds(0, slots - 1)]
        pltpu.make_async_copy(most, most, semaphore).wait()

    wait_all(recv_sem, incoming)

    @pl.loop(0, bands)
    def _(c):
        span = pl.ds(pl.multiple_of(c * lanes, lanes), lanes)
        wave = wave_ref[:, span]
        gain = jnp.where(wave == 0, 1.0, 2.0)
        live = 2 * wave < length
        cells = [incoming[c * levs + lev].astype(jnp.float32) for lev in range(levs)]
        order = [(f, lev) for f in range(FIELDS) for lev in range(levs)]
        re = jnp.concatenate([cells[lev][f : f + 1] for f, lev in order], axis=0)
        im = jnp.concatenate([cells[lev][FIELDS + f : FIELDS + f + 1] for f, lev in order], axis=0)
        re = jnp.where(live, re * gain, 0.0)
        im = jnp.where(live, im * gain, 0.0)
        for a in range(used):
            co, so = cos_out[a : a + 1, span], sin_out[a : a + 1, span]
            twist_re[a * rows : (a + 1) * rows, span] = (re * co - im * so).astype(jnp.bfloat16)
            twist_im[a * rows : (a + 1) * rows, span] = -(re * so + im * co).astype(jnp.bfloat16)

    contract = (((1,), (1,)), ((), ()))
    grid = lax.dot_general(
        twist_re[...], cos_tab[...], contract, preferred_element_type=jnp.float32
    ) + lax.dot_general(twist_im[...], sin_tab[...], contract, preferred_element_type=jnp.float32)
    lane = lax.broadcasted_iota(jnp.int32, (rows, INNER), 1)
    mixing = mixing_ref[...].astype(jnp.float32)
    updated = []
    for a in range(used):
        point = a * INNER + lane
        inside = (point < points_dev) & (base + point < length)
        cell = jnp.where(inside, grid[a * rows : (a + 1) * rows], 0.0)
        product = (cell[:levs] * cell[levs:]).astype(jnp.bfloat16).astype(jnp.float32)
        total = cell + forcing_ref[:, a * INNER : (a + 1) * INNER].astype(jnp.float32)
        for l2 in range(levs):
            total = total + mixing[:, l2 : l2 + 1] * product[l2 : l2 + 1]
        updated.append(jnp.where(inside, total, 0.0))
    updated = jnp.concatenate(updated, axis=0).astype(jnp.bfloat16)

    def send_band(band):
        @pl.loop(0, levs)
        def _(lev):
            @pl.when((band != band_id) | (lev != lev_id))
            def _():
                pltpu.make_async_remote_copy(
                    src_ref=partial.at[band * levs + lev], dst_ref=arrived.at[me],
                    send_sem=send_back, recv_sem=recv_back, device_id={"band": band, "lev": lev},
                    device_id_type=pl.DeviceIdType.MESH,
                ).start()

    @pl.loop(0, bands)
    def _(c):
        span = pl.ds(pl.multiple_of(c * lanes, lanes), lanes)
        cos_part = jnp.dot(updated, cos_tab[:, span], preferred_element_type=jnp.float32)
        sin_part = jnp.dot(updated, sin_tab[:, span], preferred_element_type=jnp.float32)
        re = jnp.zeros((rows, lanes), jnp.float32)
        im = jnp.zeros((rows, lanes), jnp.float32)
        for a in range(used):
            co, so = cos_out[a : a + 1, span], sin_out[a : a + 1, span]
            cp, sp = cos_part[a * rows : (a + 1) * rows], sin_part[a * rows : (a + 1) * rows]
            re = re + (cp * co - sp * so)
            im = im + (cp * so + sp * co)
        keep = 2 * wave_ref[:, span] < length
        re = jnp.where(keep, re * factor, 0.0)
        im = jnp.where(keep, im * -factor, 0.0)
        for lev in range(levs):
            picks = [side[f * levs + lev : f * levs + lev + 1] for side in (re, im) for f in range(FIELDS)]
            partial[c * levs + lev] = jnp.concatenate(picks, axis=0).astype(jnp.bfloat16)

        @pl.when(c > 0)
        def _():
            send_band(c - 1)

    arrived[me] = partial[me]
    send_band(bands - 1)
    wait_all(recv_back, arrived)
    sums = []
    for j in range(cycles):
        total = arrived[j * levs].astype(jnp.float32)
        for lev in range(1, levs):
            total = total + arrived[j * levs + lev].astype(jnp.float32)
        sums.append(total)
    for k in range(4):
        side = jnp.concatenate([total[k : k + 1] for total in sums], axis=0)
        for i in range(blocks):
            out_ref[i, :, k * each : (k + 1) * each] = side[:, i * each : (i + 1) * each]
    wait_all(send_sem, incoming)
    wait_all(send_back, arrived)


def on_device(spectral, legendre, cycle_len, pair_wave, quad_weight, forcing, mixing):
    band_count = lax.axis_size("band")
    lev_count = lax.axis_size("lev")
    band_id = lax.axis_index("band")
    lev_id = lax.axis_index("lev")
    pair_dev, packed = spectral.shape[3], spectral.shape[4]
    cycles = legendre.shape[1]
    levels, points_dev = forcing.shape[1], forcing.shape[3]
    rows = FIELDS * levels
    pairs = pair_block(pair_dev)
    blocks = pair_dev // pairs

    my_low = lax.dynamic_slice_in_dim(pair_wave, band_id * pair_dev, pair_dev)
    limit = (TRUNC + 1 - my_low)[:, None]
    spec_spec = pl.BlockSpec((2, FIELDS, 1, pairs, packed), lambda i: (0, 0, 0, i, 0))
    leg_spec = pl.BlockSpec((pairs, cycles, packed), lambda i: (i, 0, 0))
    limit_spec = pl.BlockSpec((pairs, 1), lambda i: (i, 0))
    cell_spec = pl.BlockSpec((1, cycles, 8 * pairs), lambda i: (i, 0, 0))
    four = pl.pallas_call(
        inverse_kernel,
        grid=(blocks,),
        in_specs=[limit_spec, spec_spec, leg_spec],
        out_specs=cell_spec,
        out_shape=jax.ShapeDtypeStruct((blocks, cycles, 8 * pairs), jnp.float32),
    )(limit, spectral, legendre)
    each_band = pl.cdiv(2 * pair_dev, 128) * 128
    low = pair_wave.reshape(band_count, blocks, 1, pairs)
    wave = jnp.concatenate([low, TRUNC - low], axis=2).reshape(band_count, 2 * pair_dev)
    dead = jnp.full((band_count, each_band - 2 * pair_dev), 1 << 14, jnp.int32)
    waves = band_count * each_band
    wave = jnp.concatenate([wave, dead], axis=1).reshape(1, waves)
    used = pl.cdiv(points_dev, INNER)
    outer = pl.cdiv(used, 8) * 8
    force = jnp.pad(forcing.reshape(rows, points_dev), ((0, 0), (0, used * INNER - points_dev)))
    vmem = pl.BlockSpec(memory_space=pltpu.VMEM)
    smem = pl.BlockSpec(memory_space=pltpu.SMEM)
    slots = band_count * lev_count
    message = pltpu.VMEM((slots, 2 * FIELDS, each_band), jnp.bfloat16)
    coeff = pl.pallas_call(
        functools.partial(grid_kernel, points_dev, lev_count),
        in_specs=[smem, smem, vmem, vmem, vmem, vmem],
        out_specs=vmem,
        out_shape=jax.ShapeDtypeStruct((blocks, cycles, 8 * pairs), jnp.float32),
        scratch_shapes=[
            pltpu.VMEM((INNER, waves), jnp.bfloat16),
            pltpu.VMEM((INNER, waves), jnp.bfloat16),
            pltpu.VMEM((outer, waves), jnp.float32),
            pltpu.VMEM((outer, waves), jnp.float32),
            pltpu.VMEM((used * rows, waves), jnp.bfloat16),
            pltpu.VMEM((used * rows, waves), jnp.bfloat16),
            pltpu.VMEM((cycles, 2 * FIELDS, each_band), jnp.bfloat16),
            message, message, message,
        ]
        + [pltpu.SemaphoreType.DMA] * 4,
        compiler_params=pltpu.CompilerParams(collective_id=0, has_side_effects=True),
    )(cycle_len, quad_weight, wave, four, force, mixing.reshape(rows, levels))
    return pl.pallas_call(
        direct_kernel,
        grid=(blocks,),
        in_specs=[limit_spec, cell_spec, leg_spec],
        out_specs=spec_spec,
        out_shape=jax.ShapeDtypeStruct(spectral.shape, jnp.bfloat16),
    )(limit, coeff, legendre)


def solution(mesh):
    return jax.shard_map(
        on_device,
        mesh=mesh,
        in_specs=(
            P(None, None, "lev", "band", None),
            P("band", None, None),
            P(),
            P(),
            P(),
            P(None, None, "band", "lev"),
            P(),
        ),
        out_specs=P(None, None, "lev", "band", None),
        check_vma=False,
    )
```

time: 66.9 us -> 45.4 us (0.68)
  Pallas kernels: 25.8 us -> 40 us
  blocking collectives: 12.2 us -> 0 us
  starting transfers between devices: 7.32 us -> 0 us
  other arithmetic: 8.05 us -> 0.89 us
  local copies, waits for them, and re-layouts: 10.1 us -> 3.73 us
  between operations: 1.45 us -> 0.04 us
  waiting for transfers between devices: 1.17 us -> 0 us
    pallas_call x1, Pallas kernels: 6.41 us -> 20.6 us  [on_device(): pl.pallas_call(functools.partial(grid_kernel, points_dev, lev_count), in_...]
    all_to_all x1 -> x0, blocking collectives: 12.2 us -> none  [on_device(): lax.all_to_all(back, ('band', 'lev'), split_axis=0, concat_axis=0, tiled=...]
    all_to_all x1 -> x0, starting transfers between devices: 7.32 us -> none  [on_device(): lax.all_to_all(four, ('band', 'lev'), split_axis=0, concat_axis=0, tiled=...]
    reshape x8 -> x1, local copies, waits for them, and re-layouts: 3.84 us -> 0.12 us  [on_device(): jnp.concatenate([low, TRUNC - low], axis=2)]
    all_to_all x3 -> x0, other arithmetic: 2.63 us -> none  [the longest x2 1.54 us: on_device(): lax.all_to_all(four, ('band', 'lev'), split_axis=0, concat_axis=0, tiled=...]
    another operation x2 -> x0, other arithmetic: 1.81 us -> none  [the longest x1 1.2 us: on_device(): scalars = jnp.stack([my_len, lev_id * points_dev])]
    convert_element_type x3 -> x0, other arithmetic: 1.81 us -> none  [the longest x1 0.78 us: on_device(): four = four.astype(jnp.bfloat16).reshape(blocks, cycles, 2, 4, pairs)]
    convert_element_type x1 -> x0, local copies, waits for them, and re-layouts: 1.72 us -> none  [on_device(): back.reshape(band_count, lev_count, 4, blocks, 2, pairs).astype(jnp.float32)]
  transfers between devices with their start and end apart: 1 -> 0, of which waited for: 1 -> 0; matrix products, arithmetic and copies ran while one was open for 8% -> 0% of each run, Pallas kernels for 0% -> 0%
where the time goes in v2:
time: 45.4 us; the launch traced here: 44.6 us
  Pallas kernels  40 us (88%)
  local copies, waits for them, and re-layouts  3.73 us (8%)
  other arithmetic  0.89 us (2%)
    pallas_call x1, Pallas kernels, on_device(): pl.pallas_call(functools.partial(grid_kernel, points_dev, lev_count), in_...  20.6 us
    pallas_call x1, Pallas kernels, on_device(): pl.pallas_call(inverse_kernel, grid=(blocks,), in_specs=[limit_spec, spec...  9.77 us
    pallas_call x1, Pallas kernels, on_device(): pl.pallas_call(direct_kernel, grid=(blocks,), in_specs=[limit_spec, cell_...  9.62 us

profile of v2, /device:TPU:0, one launch (start us, length us, event | category | flops | bytes accessed | tf_op | source)
XLA Modules:
  0.0 44.6 jit_solution(10743751442887812870)
XLA Ops:
  0.0 0.8 %dynamic-slice_subtract_fusion = s32[160]{0:T(256)S(1)} fusion(s32[1280]{0:T(1024)} %param.10, s32[]{:T(128)S(6)} %select_n.3), kind=kLoop, calls=%fused_computation.3 | loop fusion | flops 160 | bytes 1284 | tf_op jit(solution)/shard_map/sub | solution.py:265
  0.8 0.8 %reshape.27 = s32[8,10,1,16]{3,2,1,0:T(1,128)S(1)} reshape(s32[1280]{0:T(1024)} %param.10) | data formatting | bytes 10240 | tf_op jit(solution)/shard_map/reshape | solution.py:278
  1.6 0.1 pad_add_fusion
  1.7 0.1 reshape.28
  1.9 0.6 %copy.15 = s32[1,1,8,384]{3,1,2,0:T(1,128)} copy(s32[1,1,8,384]{3,2,1,0:T(8,128)S(1)} %pad_bitcast_fusion) | data formatting | bytes 24576
  2.5 0.8 %reshape.30 = bf16[8,2564]{1,0:T(8,128)(2,1)S(1)} reshape(bf16[2,4,1,2564]{3,1,2,0:T(4,128)(2,1)} %param.12) | data formatting | bytes 82048 | tf_op jit(solution)/shard_map/reshape | solution.py:285
  3.3 0.6 %pad.5.forcing_ref = bf16[8,2816]{1,0:T(8,128)(2,1)} pad(bf16[8,2564]{1,0:T(8,128)(2,1)S(1)} %reshape.30, bf16[]{:T(256)} %constant.19.clone.1), padding=0_0x0_252 | pad | bytes 86082 | tf_op jit(solution)/shard_map/jit(_pad)/pad | solution.py:285
  3.9 0.7 %copy.13.limit_ref = s32[160,1]{1,0:T(8,128)} copy(s32[160,1]{0,1:T(1,128)S(1)} %bitcast.9) | data formatting | bytes 1280 | tf_op jit(solution)/shard_map/broadcast_in_dim | solution.py:265
  4.6 9.8 %shard_map.73.four_ref = f32[10,8,128]{2,1,0:T(8,128)} custom-call(s32[160,1]{1,0:T(8,128)} %copy.13.limit_ref, bf16[2,2,1,160,2561]{4,3,2,1,0:T(8,128)(2,1)} %spec_ref.1, bf16[160,8,2561]{2,1,0:T(8,128)(2,1)} %leg_ref.3), custom_call_target="tpu_custom_call" | custom-call | tf_op jit(solution)/shard_map/pallas_call | solution.py:270
  14.4 20.6 %shard_map.74.coeff_ref = f32[10,8,128]{2,1,0:T(8,128)} custom-call(s32[8]{0:T(128)} %length_ref.1, f32[8]{0:T(128)} %weight_ref.1, s32[1,3072]{1,0:T(1,128)} %bitcast.8, f32[10,8,128]{2,1,0:T(8,128)} %shard_map.73.four_ref, bf16[8,2816]{1,0:T(8,128)(2,1)} %pad.5.forcing_ref, bf16[8,4]{1,0:T(8,128)(2,1)} %bitcast.10), custom_call_target="tpu_custom_call" | custom-call | tf_op jit(solution)/shard_map/pallas_call | solution.py:290
  35.0 9.6 %shard_map.75 = bf16[2,2,1,160,2561]{4,3,2,1,0:T(8,128)(2,1)} custom-call(s32[160,1]{1,0:T(8,128)} %copy.13.limit_ref, f32[10,8,128]{2,1,0:T(8,128)} %shard_map.74.coeff_ref, bf16[160,8,2561]{2,1,0:T(8,128)(2,1)} %leg_ref.3), custom_call_target="tpu_custom_call" | custom-call | tf_op jit(solution)/shard_map/pallas_call | solution.py:308
  (2 shorter events, 0.0 us)

commit v3 on v2

--- a/solution.py
+++ b/solution.py
@@ -43,48 +43,70 @@
     return rows == lanes
 
 
-def inverse_kernel(limit_ref, spec_ref, leg_ref, out_ref):
-    pairs, cycles, packed = leg_ref.shape
+def read_chunk(leg_hbm, leg_vmem, sem, pairs, i):
+    part = pl.ds(pl.multiple_of(i * pairs, pairs), pairs)
+    return pltpu.make_async_copy(leg_hbm.at[part], leg_vmem.at[part], sem.at[i])
+
+
+def direct_kernel(limit_ref, coeff_ref, leg_hbm, out_hbm, leg_vmem, out_vmem, in_sem, out_sem):
+    blocks, cycles, wide_lanes = coeff_ref.shape
+    pairs = wide_lanes // 8
+    packed = leg_vmem.shape[2]
+
+    def write(i):
+        part = pl.ds(pl.multiple_of(i * pairs, pairs), pairs)
+        return pltpu.make_async_copy(
+            out_vmem.at[:, :, :, part], out_hbm.at[:, :, :, part], out_sem.at[i]
+        )
+
+    for i in range(blocks):
+        read_chunk(leg_hbm, leg_vmem, in_sem, pairs, i).start()
+    mask = diagonal(pairs, cycles)
     column = lax.broadcasted_iota(jnp.int32, (pairs, packed), 1)
-    lower = column < limit_ref[...]
-    halves = []
-    for s in range(2):
-        for f in range(FIELDS):
-            row = spec_ref[s, f, 0].astype(jnp.float32)
-            halves += [jnp.where(lower, row, 0.0), jnp.where(lower, 0.0, row)]
-    spec = jnp.concatenate(halves, axis=0).astype(jnp.bfloat16)
-    leg = leg_ref[...].reshape(pairs * cycles, packed)
-    full = lax.dot_general(
-        leg, spec, (((1,), (1,)), ((), ())), preferred_element_type=jnp.float32
-    )
-    full = full.reshape(pairs, cycles, 8 * pairs)
-    out_ref[0] = jnp.sum(jnp.where(diagonal(pairs, cycles), full, 0.0), axis=0)
-
-
-def direct_kernel(limit_ref, coeff_ref, leg_ref, out_ref):
-    pairs, cycles, packed = leg_ref.shape
-    wide = jnp.broadcast_to(coeff_ref[...], (pairs, cycles, 8 * pairs))
-    wide = jnp.where(diagonal(pairs, cycles), wide, 0.0).reshape(pairs * cycles, 8 * pairs)
-    wide = wide.T.astype(jnp.bfloat16)
-    leg = leg_ref[...].reshape(pairs * cycles, packed)
-    full = jnp.dot(wide, leg, preferred_element_type=jnp.float32)
-    column = lax.broadcasted_iota(jnp.int32, (pairs, packed), 1)
-    lower = column < limit_ref[...]
-    for s in range(2):
-        for f in range(FIELDS):
-            at = (s * FIELDS + f) * 2 * pairs
-            low = full[at : at + pairs]
-            high = full[at + pairs : at + 2 * pairs]
-            out_ref[s, f, 0] = jnp.where(lower, low, high).astype(jnp.bfloat16)
+
+    @pl.loop(0, blocks)
+    def _(i):
+        part = pl.ds(pl.multiple_of(i * pairs, pairs), pairs)
+        wide = jnp.broadcast_to(coeff_ref[pl.ds(i, 1)], (pairs, cycles, 8 * pairs))
+        wide = jnp.where(mask, wide, 0.0).reshape(pairs * cycles, 8 * pairs)
+        wide = wide.T.astype(jnp.bfloat16)
+        lower = column < limit_ref[part]
+        read_chunk(leg_hbm, leg_vmem, in_sem, pairs, i).wait()
+        leg = leg_vmem[part].reshape(pairs * cycles, packed)
+        full = jnp.dot(wide, leg, preferred_element_type=jnp.float32)
+        for s in range(2):
+            for f in range(FIELDS):
+                at = (s * FIELDS + f) * 2 * pairs
+                low = full[at : at + pairs]
+                high = full[at + pairs : at + 2 * pairs]
+                out_vmem[s, f, 0, part] = jnp.where(lower, low, high).astype(jnp.bfloat16)
+        write(i).start()
+
+    for i in range(blocks):
+        write(i).wait()
 
 
 def grid_kernel(
-    points_dev, levs, length_ref, weight_ref, wave_ref, four_ref, forcing_ref, mixing_ref, out_ref,
+    points_dev, levs, length_ref, weight_ref, low_ref, forcing_ref, mixing_ref, spec_hbm, leg_hbm,
+    out_ref, limit_ref,
     cos_tab, sin_tab, cos_out, sin_out, twist_re, twist_im,
-    outgoing, incoming, partial, arrived, send_sem, recv_sem, send_back, recv_back,
+    outgoing, incoming, partial, arrived, leg_vmem, spec_vmem, four_ref, wave_ref,
+    send_sem, recv_sem, send_back, recv_back, leg_sem, spec_sem,
 ):
     blocks, cycles, wide = four_ref.shape
+    pairs = wide // 8
+    packed = leg_vmem.shape[2]
     each = wide // 4
+
+    def read_spec(i):
+        part = pl.ds(pl.multiple_of(i * pairs, pairs), pairs)
+        return pltpu.make_async_copy(
+            spec_hbm.at[:, :, :, part], spec_vmem.at[:, :, :, part], spec_sem.at[i]
+        )
+
+    for i in range(blocks):
+        read_spec(i).start()
+        read_chunk(leg_hbm, leg_vmem, leg_sem, pairs, i).start()
     rows = FIELDS * levs
     outer = cos_out.shape[0]
     used = pl.cdiv(points_dev, INNER)
@@ -111,19 +133,22 @@
             barrier, inc=1, device_id={"band": band, "lev": lev}, device_id_type=pl.DeviceIdType.MESH
         )
 
-    sides = []
-    for k in range(4):
-        parts = [four_ref[i, :, k * each : (k + 1) * each] for i in range(blocks)]
-        if lanes > blocks * each:
-            parts.append(jnp.zeros((cycles, lanes - blocks * each), jnp.float32))
-        sides.append(jnp.concatenate(parts, axis=1))
-    for j in range(cycles):
-        block = jnp.concatenate([side[j : j + 1] for side in sides], axis=0)
-        outgoing[j] = block.astype(jnp.bfloat16)
+    parts = []
+    for i in range(blocks):
+        low = low_ref[:, i * pairs : (i + 1) * pairs]
+        parts += [low, TRUNC - low]
+    if lanes > blocks * each:
+        parts.append(jnp.full((bands, lanes - blocks * each), 1 << 14, jnp.int32))
+    wave_ref[...] = jnp.concatenate(parts, axis=1)
+    mine = jnp.broadcast_to(wave_ref[pl.ds(band_id, 1), :].astype(jnp.float32), (8, lanes)).T
+    for i in range(blocks):
+        limit_ref[i * pairs : (i + 1) * pairs] = TRUNC + 1 - mine[
+            i * each : i * each + pairs, 0:1
+        ].astype(jnp.int32)
 
     def tables(c):
         span = pl.ds(pl.multiple_of(c * lanes, lanes), lanes)
-        wave = wave_ref[:, span]
+        wave = wave_ref[pl.ds(c, 1), :]
         eight = lax.broadcasted_iota(jnp.int32, (8, lanes), 0)
         c0, s0 = sincos(wave, eight, length, inverse_length)
         c1, s1 = sincos(wave, eight * 8, length, inverse_length)
@@ -143,6 +168,38 @@
 
     early = bands // 2
     pl.loop(0, early)(tables)
+    mask = diagonal(pairs, cycles)
+    column = lax.broadcasted_iota(jnp.int32, (pairs, packed), 1)
+
+    @pl.loop(0, blocks)
+    def _(i):
+        part = pl.ds(pl.multiple_of(i * pairs, pairs), pairs)
+        lower = column < limit_ref[part]
+        read_spec(i).wait()
+        halves = []
+        for s in range(2):
+            for f in range(FIELDS):
+                row = spec_vmem[s, f, 0, part].astype(jnp.float32)
+                halves += [jnp.where(lower, row, 0.0), jnp.where(lower, 0.0, row)]
+        spec = jnp.concatenate(halves, axis=0).astype(jnp.bfloat16)
+        read_chunk(leg_hbm, leg_vmem, leg_sem, pairs, i).wait()
+        leg = leg_vmem[part].reshape(pairs * cycles, packed)
+        full = lax.dot_general(
+            leg, spec, (((1,), (1,)), ((), ())), preferred_element_type=jnp.float32
+        )
+        full = full.reshape(pairs, cycles, 8 * pairs)
+        four_ref[i] = jnp.sum(jnp.where(mask, full, 0.0), axis=0)
+
+    sides = []
+    for k in range(4):
+        parts = [four_ref[i, :, k * each : (k + 1) * each] for i in range(blocks)]
+        if lanes > blocks * each:
+            parts.append(jnp.zeros((cycles, lanes - blocks * each), jnp.float32))
+        sides.append(jnp.concatenate(parts, axis=1))
+    for j in range(cycles):
+        block = jnp.concatenate([side[j : j + 1] for side in sides], axis=0)
+        outgoing[j] = block.astype(jnp.bfloat16)
+
     pl.semaphore_wait(barrier, slots - 1)
 
     @pl.loop(1, slots)
@@ -166,7 +223,7 @@
     @pl.loop(0, bands)
     def _(c):
         span = pl.ds(pl.multiple_of(c * lanes, lanes), lanes)
-        wave = wave_ref[:, span]
+        wave = wave_ref[pl.ds(c, 1), :]
         gain = jnp.where(wave == 0, 1.0, 2.0)
         live = 2 * wave < length
         cells = [incoming[c * levs + lev].astype(jnp.float32) for lev in range(levs)]
@@ -221,7 +278,7 @@
             cp, sp = cos_part[a * rows : (a + 1) * rows], sin_part[a * rows : (a + 1) * rows]
             re = re + (cp * co - sp * so)
             im = im + (cp * so + sp * co)
-        keep = 2 * wave_ref[:, span] < length
+        keep = 2 * wave_ref[pl.ds(c, 1), :] < length
         re = jnp.where(keep, re * factor, 0.0)
         im = jnp.where(keep, im * -factor, 0.0)
         for lev in range(levs):
@@ -252,34 +309,15 @@
 def on_device(spectral, legendre, cycle_len, pair_wave, quad_weight, forcing, mixing):
     band_count = lax.axis_size("band")
     lev_count = lax.axis_size("lev")
-    band_id = lax.axis_index("band")
-    lev_id = lax.axis_index("lev")
-    pair_dev, packed = spectral.shape[3], spectral.shape[4]
+    pair_dev = spectral.shape[3]
     cycles = legendre.shape[1]
     levels, points_dev = forcing.shape[1], forcing.shape[3]
     rows = FIELDS * levels
     pairs = pair_block(pair_dev)
     blocks = pair_dev // pairs
 
-    my_low = lax.dynamic_slice_in_dim(pair_wave, band_id * pair_dev, pair_dev)
-    limit = (TRUNC + 1 - my_low)[:, None]
-    spec_spec = pl.BlockSpec((2, FIELDS, 1, pairs, packed), lambda i: (0, 0, 0, i, 0))
-    leg_spec = pl.BlockSpec((pairs, cycles, packed), lambda i: (i, 0, 0))
-    limit_spec = pl.BlockSpec((pairs, 1), lambda i: (i, 0))
-    cell_spec = pl.BlockSpec((1, cycles, 8 * pairs), lambda i: (i, 0, 0))
-    four = pl.pallas_call(
-        inverse_kernel,
-        grid=(blocks,),
-        in_specs=[limit_spec, spec_spec, leg_spec],
-        out_specs=cell_spec,
-        out_shape=jax.ShapeDtypeStruct((blocks, cycles, 8 * pairs), jnp.float32),
-    )(limit, spectral, legendre)
     each_band = pl.cdiv(2 * pair_dev, 128) * 128
-    low = pair_wave.reshape(band_count, blocks, 1, pairs)
-    wave = jnp.concatenate([low, TRUNC - low], axis=2).reshape(band_count, 2 * pair_dev)
-    dead = jnp.full((band_count, each_band - 2 * pair_dev), 1 << 14, jnp.int32)
     waves = band_count * each_band
-    wave = jnp.concatenate([wave, dead], axis=1).reshape(1, waves)
     used = pl.cdiv(points_dev, INNER)
     outer = pl.cdiv(used, 8) * 8
     force = jnp.pad(forcing.reshape(rows, points_dev), ((0, 0), (0, used * INNER - points_dev)))
@@ -287,11 +325,15 @@
     smem = pl.BlockSpec(memory_space=pltpu.SMEM)
     slots = band_count * lev_count
     message = pltpu.VMEM((slots, 2 * FIELDS, each_band), jnp.bfloat16)
-    coeff = pl.pallas_call(
+    hbm = pl.BlockSpec(memory_space=pl.ANY)
+    coeff, limit = pl.pallas_call(
         functools.partial(grid_kernel, points_dev, lev_count),
-        in_specs=[smem, smem, vmem, vmem, vmem, vmem],
-        out_specs=vmem,
-        out_shape=jax.ShapeDtypeStruct((blocks, cycles, 8 * pairs), jnp.float32),
+        in_specs=[smem, smem, vmem, vmem, vmem, hbm, hbm],
+        out_specs=[vmem, vmem],
+        out_shape=[
+            jax.ShapeDtypeStruct((blocks, cycles, 8 * pairs), jnp.float32),
+            jax.ShapeDtypeStruct((pair_dev, 1), jnp.int32),
+        ],
         scratch_shapes=[
             pltpu.VMEM((INNER, waves), jnp.bfloat16),
             pltpu.VMEM((INNER, waves), jnp.bfloat16),
@@ -301,16 +343,28 @@
             pltpu.VMEM((used * rows, waves), jnp.bfloat16),
             pltpu.VMEM((cycles, 2 * FIELDS, each_band), jnp.bfloat16),
             message, message, message,
+            pltpu.VMEM(legendre.shape, jnp.bfloat16),
+            pltpu.VMEM(spectral.shape, jnp.bfloat16),
+            pltpu.VMEM((blocks, cycles, 8 * pairs), jnp.float32),
+            pltpu.VMEM((band_count, each_band), jnp.int32),
         ]
-        + [pltpu.SemaphoreType.DMA] * 4,
+        + [pltpu.SemaphoreType.DMA] * 4
+        + [pltpu.SemaphoreType.DMA((blocks,))] * 2,
         compiler_params=pltpu.CompilerParams(collective_id=0, has_side_effects=True),
-    )(cycle_len, quad_weight, wave, four, force, mixing.reshape(rows, levels))
+    )(
+        cycle_len, quad_weight, pair_wave.reshape(band_count, pair_dev), force,
+        mixing.reshape(rows, levels), spectral, legendre,
+    )
     return pl.pallas_call(
         direct_kernel,
-        grid=(blocks,),
-        in_specs=[limit_spec, cell_spec, leg_spec],
-        out_specs=spec_spec,
+        in_specs=[vmem, vmem, hbm],
+        out_specs=hbm,
         out_shape=jax.ShapeDtypeStruct(spectral.shape, jnp.bfloat16),
+        scratch_shapes=[
+            pltpu.VMEM(legendre.shape, jnp.bfloat16),
+            pltpu.VMEM(spectral.shape, jnp.bfloat16),
+        ]
+        + [pltpu.SemaphoreType.DMA((blocks,))] * 2,
     )(limit, coeff, legendre)
 
 

time: 45.4 us -> 32.6 us (0.72)
  Pallas kernels: 40 us -> 29.5 us
  local copies, waits for them, and re-layouts: 3.73 us -> 2.8 us
  other arithmetic: 0.89 us -> 0 us
    pallas_call x2 -> x1, Pallas kernels: 19.4 us -> 7.12 us  [on_device(): pl.pallas_call(direct_kernel, in_specs=[vmem, vmem, hbm], out_specs=hbm,...]
    pallas_call x1, Pallas kernels: 20.6 us -> 22.3 us  [on_device(): pl.pallas_call(functools.partial(grid_kernel, points_dev, lev_count), in_...]
    sub x2 -> x0, other arithmetic: 0.81 us -> none  [the longest x1 0.77 us: on_device(): limit = (TRUNC + 1 - my_low)[:, None]]
    broadcast_in_dim x1 -> x0, local copies, waits for them, and re-layouts: 0.74 us -> none  [on_device(): limit = (TRUNC + 1 - my_low)[:, None]]
    unnamed x2 -> x0, local copies, waits for them, and re-layouts: 0.62 us -> none
    reshape x2 -> x1, local copies, waits for them, and re-layouts: 0.93 us -> 1.36 us  [on_device(): pair_wave.reshape(band_count, pair_dev)]
where the time goes in v3:
time: 32.6 us; the launch traced here: 32.3 us
  Pallas kernels  29.5 us (90%)
  local copies, waits for them, and re-layouts  2.8 us (9%)
    pallas_call x1, Pallas kernels, on_device(): pl.pallas_call(functools.partial(grid_kernel, points_dev, lev_count), in_...  22.3 us
    pallas_call x1, Pallas kernels, on_device(): pl.pallas_call(direct_kernel, in_specs=[vmem, vmem, hbm], out_specs=hbm,...  7.12 us
    reshape x1, local copies, waits for them, and re-layouts, on_device(): pair_wave.reshape(band_count, pair_dev)  1.36 us
    reshape x1, local copies, waits for them, and re-layouts, on_device(): forcing.reshape(rows, points_dev)  0.81 us

profile of v3, /device:TPU:0, one launch (start us, length us, event | category | flops | bytes accessed | tf_op | source)
XLA Modules:
  0.0 32.3 jit_solution(9954314912329097545)
XLA Ops:
  0.0 1.4 %reshape.9.low_ref = s32[8,160]{1,0:T(8,128)} reshape(s32[1280]{0:T(1024)} %param.10) | data formatting | bytes 10240 | tf_op jit(solution)/shard_map/reshape | solution.py:355
  1.4 0.8 %reshape.10 = bf16[8,2564]{1,0:T(8,128)(2,1)S(1)} reshape(bf16[2,4,1,2564]{3,1,2,0:T(4,128)(2,1)} %param.12) | data formatting | bytes 82048 | tf_op jit(solution)/shard_map/reshape | solution.py:323
  2.2 0.6 %pad.4.forcing_ref = bf16[8,2816]{1,0:T(8,128)(2,1)} pad(bf16[8,2564]{1,0:T(8,128)(2,1)S(1)} %reshape.10, bf16[]{:T(256)} %constant.2.clone.1), padding=0_0x0_252 | pad | bytes 86082 | tf_op jit(solution)/shard_map/jit(_pad)/pad | solution.py:323
  2.8 22.3 %shard_map.73 = (f32[10,8,128]{2,1,0:T(8,128)}, s32[160,1]{1,0:T(8,128)}) custom-call(s32[8]{0:T(128)} %length_ref.1, f32[8]{0:T(128)} %weight_ref.1, s32[8,160]{1,0:T(8,128)} %reshape.9.low_ref, bf16[8,2816]{1,0:T(8,128)(2,1)} %pad.4.forcing_ref, bf16[8,4]{1,0:T(8,128)(2,1)} %bitcast.3, bf16[2,2,1,160,2561]{4,3,2,1,0:T(8,128)(2,1)} %spec_hbm.1, ...), custom_call_target="tpu_custom_call" | custom-call | tf_op jit(solution)/shard_map/pallas_call | solution.py:329
  25.2 7.1 %shard_map.74 = bf16[2,2,1,160,2561]{4,3,2,1,0:T(8,128)(2,1)} custom-call(s32[160,1]{1,0:T(8,128)} %get-tuple-element.7.limit_ref, f32[10,8,128]{2,1,0:T(8,128)} %get-tuple-element.8.coeff_ref, bf16[160,8,2561]{2,1,0:T(8,128)(2,1)} %leg_hbm.3), custom_call_target="tpu_custom_call" | custom-call | tf_op jit(solution)/shard_map/pallas_call | solution.py:358

commit v4 on v3

--- a/solution.py
+++ b/solution.py
@@ -48,7 +48,7 @@
     return pltpu.make_async_copy(leg_hbm.at[part], leg_vmem.at[part], sem.at[i])
 
 
-def direct_kernel(limit_ref, coeff_ref, leg_hbm, out_hbm, leg_vmem, out_vmem, in_sem, out_sem):
+def direct_kernel(split, limit_ref, coeff_ref, leg_hbm, out_hbm, leg_vmem, out_vmem, in_sem, out_sem):
     blocks, cycles, wide_lanes = coeff_ref.shape
     pairs = wide_lanes // 8
     packed = leg_vmem.shape[2]
@@ -62,7 +62,8 @@
     for i in range(blocks):
         read_chunk(leg_hbm, leg_vmem, in_sem, pairs, i).start()
     mask = diagonal(pairs, cycles)
-    column = lax.broadcasted_iota(jnp.int32, (pairs, packed), 1)
+    column = split + lax.broadcasted_iota(jnp.int32, (pairs, packed - split), 1)
+    half = 4 * pairs
 
     @pl.loop(0, blocks)
     def _(i):
@@ -73,13 +74,14 @@
         lower = column < limit_ref[part]
         read_chunk(leg_hbm, leg_vmem, in_sem, pairs, i).wait()
         leg = leg_vmem[part].reshape(pairs * cycles, packed)
-        full = jnp.dot(wide, leg, preferred_element_type=jnp.float32)
+        left = jnp.dot(wide[:half], leg[:, :split], preferred_element_type=jnp.float32)
+        right = jnp.dot(wide, leg[:, split:], preferred_element_type=jnp.float32)
         for s in range(2):
             for f in range(FIELDS):
-                at = (s * FIELDS + f) * 2 * pairs
-                low = full[at : at + pairs]
-                high = full[at + pairs : at + 2 * pairs]
-                out_vmem[s, f, 0, part] = jnp.where(lower, low, high).astype(jnp.bfloat16)
+                at = (s * FIELDS + f) * pairs
+                out_vmem[s, f, 0, part, :split] = left[at : at + pairs].astype(jnp.bfloat16)
+                low, high = right[at : at + pairs], right[half + at : half + at + pairs]
+                out_vmem[s, f, 0, part, split:] = jnp.where(lower, low, high).astype(jnp.bfloat16)
         write(i).start()
 
     for i in range(blocks):
@@ -87,7 +89,7 @@
 
 
 def grid_kernel(
-    points_dev, levs, length_ref, weight_ref, low_ref, forcing_ref, mixing_ref, spec_hbm, leg_hbm,
+    points_dev, levs, split, length_ref, weight_ref, low_ref, forcing_ref, mixing_ref, spec_hbm, leg_hbm,
     out_ref, limit_ref,
     cos_tab, sin_tab, cos_out, sin_out, twist_re, twist_im,
     outgoing, incoming, partial, arrived, leg_vmem, spec_vmem, four_ref, wave_ref,
@@ -133,18 +135,12 @@
             barrier, inc=1, device_id={"band": band, "lev": lev}, device_id_type=pl.DeviceIdType.MESH
         )
 
-    parts = []
-    for i in range(blocks):
-        low = low_ref[:, i * pairs : (i + 1) * pairs]
-        parts += [low, TRUNC - low]
+    parts = [low_ref[...], TRUNC - low_ref[...]]
     if lanes > blocks * each:
         parts.append(jnp.full((bands, lanes - blocks * each), 1 << 14, jnp.int32))
     wave_ref[...] = jnp.concatenate(parts, axis=1)
     mine = jnp.broadcast_to(wave_ref[pl.ds(band_id, 1), :].astype(jnp.float32), (8, lanes)).T
-    for i in range(blocks):
-        limit_ref[i * pairs : (i + 1) * pairs] = TRUNC + 1 - mine[
-            i * each : i * each + pairs, 0:1
-        ].astype(jnp.int32)
+    limit_ref[...] = TRUNC + 1 - mine[: blocks * pairs, 0:1].astype(jnp.int32)
 
     def tables(c):
         span = pl.ds(pl.multiple_of(c * lanes, lanes), lanes)
@@ -169,30 +165,38 @@
     early = bands // 2
     pl.loop(0, early)(tables)
     mask = diagonal(pairs, cycles)
-    column = lax.broadcasted_iota(jnp.int32, (pairs, packed), 1)
+    column = split + lax.broadcasted_iota(jnp.int32, (pairs, packed - split), 1)
+    inner = (((1,), (1,)), ((), ()))
 
     @pl.loop(0, blocks)
     def _(i):
         part = pl.ds(pl.multiple_of(i * pairs, pairs), pairs)
         lower = column < limit_ref[part]
         read_spec(i).wait()
-        halves = []
+        whole, lows, highs = [], [], []
         for s in range(2):
             for f in range(FIELDS):
-                row = spec_vmem[s, f, 0, part].astype(jnp.float32)
-                halves += [jnp.where(lower, row, 0.0), jnp.where(lower, 0.0, row)]
-        spec = jnp.concatenate(halves, axis=0).astype(jnp.bfloat16)
+                whole.append(spec_vmem[s, f, 0, part, :split])
+                row = spec_vmem[s, f, 0, part, split:].astype(jnp.float32)
+                lows.append(jnp.where(lower, row, 0.0))
+                highs.append(jnp.where(lower, 0.0, row))
+        left = jnp.concatenate(whole, axis=0)
+        right = jnp.concatenate(lows + highs, axis=0).astype(jnp.bfloat16)
         read_chunk(leg_hbm, leg_vmem, leg_sem, pairs, i).wait()
         leg = leg_vmem[part].reshape(pairs * cycles, packed)
-        full = lax.dot_general(
-            leg, spec, (((1,), (1,)), ((), ())), preferred_element_type=jnp.float32
-        )
+        full = lax.dot_general(leg[:, split:], right, inner, preferred_element_type=jnp.float32)
+        some = lax.dot_general(leg[:, :split], left, inner, preferred_element_type=jnp.float32)
+        full = full + jnp.concatenate([some, jnp.zeros_like(some)], axis=1)
         full = full.reshape(pairs, cycles, 8 * pairs)
         four_ref[i] = jnp.sum(jnp.where(mask, full, 0.0), axis=0)
 
     sides = []
     for k in range(4):
-        parts = [four_ref[i, :, k * each : (k + 1) * each] for i in range(blocks)]
+        parts = [
+            four_ref[i, :, (4 * h + k) * pairs : (4 * h + k + 1) * pairs]
+            for h in range(2)
+            for i in range(blocks)
+        ]
         if lanes > blocks * each:
             parts.append(jnp.zeros((cycles, lanes - blocks * each), jnp.float32))
         sides.append(jnp.concatenate(parts, axis=1))
@@ -300,8 +304,10 @@
         sums.append(total)
     for k in range(4):
         side = jnp.concatenate([total[k : k + 1] for total in sums], axis=0)
-        for i in range(blocks):
-            out_ref[i, :, k * each : (k + 1) * each] = side[:, i * each : (i + 1) * each]
+        for h in range(2):
+            for i in range(blocks):
+                at, lane = (4 * h + k) * pairs, (h * blocks + i) * pairs
+                out_ref[i, :, at : at + pairs] = side[:, lane : lane + pairs]
     wait_all(send_sem, incoming)
     wait_all(send_back, arrived)
 
@@ -325,9 +331,10 @@
     smem = pl.BlockSpec(memory_space=pltpu.SMEM)
     slots = band_count * lev_count
     message = pltpu.VMEM((slots, 2 * FIELDS, each_band), jnp.bfloat16)
+    split = (TRUNC + 2 - pair_wave.shape[0]) // 128 * 128
     hbm = pl.BlockSpec(memory_space=pl.ANY)
     coeff, limit = pl.pallas_call(
-        functools.partial(grid_kernel, points_dev, lev_count),
+        functools.partial(grid_kernel, points_dev, lev_count, split),
         in_specs=[smem, smem, vmem, vmem, vmem, hbm, hbm],
         out_specs=[vmem, vmem],
         out_shape=[
@@ -356,7 +363,7 @@
         mixing.reshape(rows, levels), spectral, legendre,
     )
     return pl.pallas_call(
-        direct_kernel,
+        functools.partial(direct_kernel, split),
         in_specs=[vmem, vmem, hbm],
         out_specs=hbm,
         out_shape=jax.ShapeDtypeStruct(spectral.shape, jnp.bfloat16),

time: 32.6 us -> 31.9 us (0.979)
  Pallas kernels: 29.5 us -> 28.7 us
    pallas_call x2, Pallas kernels: 29.5 us -> 28.7 us  [the longest x1 21.9 us: on_device(): pl.pallas_call(functools.partial(grid_kernel, points_dev, lev_count, spli...]
where the time goes in v4:
time: 31.9 us; the launch traced here: 31.5 us
  Pallas kernels  28.7 us (90%)
  local copies, waits for them, and re-layouts  2.8 us (9%)
    pallas_call x1, Pallas kernels, on_device(): pl.pallas_call(functools.partial(grid_kernel, points_dev, lev_count, spli...  21.9 us
    pallas_call x1, Pallas kernels, on_device(): pl.pallas_call(functools.partial(direct_kernel, split), in_specs=[vmem, v...  6.8 us
    reshape x1, local copies, waits for them, and re-layouts, on_device(): pair_wave.reshape(band_count, pair_dev)  1.36 us
    reshape x1, local copies, waits for them, and re-layouts, on_device(): forcing.reshape(rows, points_dev)  0.81 us

profile of v4, /device:TPU:0, one launch (start us, length us, event | category | flops | bytes accessed | tf_op | source)
XLA Modules:
  0.0 31.5 jit_solution(5287144569134239844)
XLA Ops:
  0.0 1.4 %reshape.9.low_ref = s32[8,160]{1,0:T(8,128)} reshape(s32[1280]{0:T(1024)} %param.10) | data formatting | bytes 10240 | tf_op jit(solution)/shard_map/reshape | solution.py:362
  1.4 0.8 %reshape.10 = bf16[8,2564]{1,0:T(8,128)(2,1)S(1)} reshape(bf16[2,4,1,2564]{3,1,2,0:T(4,128)(2,1)} %param.12) | data formatting | bytes 82048 | tf_op jit(solution)/shard_map/reshape | solution.py:329
  2.2 0.6 %pad.4.forcing_ref = bf16[8,2816]{1,0:T(8,128)(2,1)} pad(bf16[8,2564]{1,0:T(8,128)(2,1)S(1)} %reshape.10, bf16[]{:T(256)} %constant.2.clone.1), padding=0_0x0_252 | pad | bytes 86082 | tf_op jit(solution)/shard_map/jit(_pad)/pad | solution.py:329
  2.8 21.9 %shard_map.73 = (f32[10,8,128]{2,1,0:T(8,128)}, s32[160,1]{1,0:T(8,128)}) custom-call(s32[8]{0:T(128)} %length_ref.1, f32[8]{0:T(128)} %weight_ref.1, s32[8,160]{1,0:T(8,128)} %reshape.9.low_ref, bf16[8,2816]{1,0:T(8,128)(2,1)} %pad.4.forcing_ref, bf16[8,4]{1,0:T(8,128)(2,1)} %bitcast.3, bf16[2,2,1,160,2561]{4,3,2,1,0:T(8,128)(2,1)} %spec_hbm.1, ...), custom_call_target="tpu_custom_call" | custom-call | tf_op jit(solution)/shard_map/pallas_call | solution.py:336
  24.7 6.8 %shard_map.74 = bf16[2,2,1,160,2561]{4,3,2,1,0:T(8,128)(2,1)} custom-call(s32[160,1]{1,0:T(8,128)} %get-tuple-element.7.limit_ref, f32[10,8,128]{2,1,0:T(8,128)} %get-tuple-element.8.coeff_ref, bf16[160,8,2561]{2,1,0:T(8,128)(2,1)} %leg_hbm.3), custom_call_target="tpu_custom_call" | custom-call | tf_op jit(solution)/shard_map/pallas_call | solution.py:365

commit v5 on v4

--- a/solution.py
+++ b/solution.py
@@ -135,7 +135,9 @@
             barrier, inc=1, device_id={"band": band, "lev": lev}, device_id_type=pl.DeviceIdType.MESH
         )
 
-    parts = [low_ref[...], TRUNC - low_ref[...]]
+    own = blocks * pairs
+    low = jnp.concatenate([low_ref[:, k * own : (k + 1) * own] for k in range(bands)], axis=0)
+    parts = [low, TRUNC - low]
     if lanes > blocks * each:
         parts.append(jnp.full((bands, lanes - blocks * each), 1 << 14, jnp.int32))
     wave_ref[...] = jnp.concatenate(parts, axis=1)
@@ -260,8 +262,10 @@
     updated = jnp.concatenate(updated, axis=0).astype(jnp.bfloat16)
 
     def send_band(band):
-        @pl.loop(0, levs)
-        def _(lev):
+        @pl.loop(1, levs + 1)
+        def _(turn):
+            lev = (lev_id + turn) % levs
+
             @pl.when((band != band_id) | (lev != lev_id))
             def _():
                 pltpu.make_async_remote_copy(
@@ -271,7 +275,8 @@
                 ).start()
 
     @pl.loop(0, bands)
-    def _(c):
+    def _(turn):
+        c = (band_id + 1 + turn) % bands
         span = pl.ds(pl.multiple_of(c * lanes, lanes), lanes)
         cos_part = jnp.dot(updated, cos_tab[:, span], preferred_element_type=jnp.float32)
         sin_part = jnp.dot(updated, sin_tab[:, span], preferred_element_type=jnp.float32)
@@ -289,12 +294,12 @@
             picks = [side[f * levs + lev : f * levs + lev + 1] for side in (re, im) for f in range(FIELDS)]
             partial[c * levs + lev] = jnp.concatenate(picks, axis=0).astype(jnp.bfloat16)
 
-        @pl.when(c > 0)
+        @pl.when(turn > 0)
         def _():
-            send_band(c - 1)
+            send_band((band_id + turn) % bands)
 
     arrived[me] = partial[me]
-    send_band(bands - 1)
+    send_band(band_id)
     wait_all(recv_back, arrived)
     sums = []
     for j in range(cycles):
@@ -359,7 +364,7 @@
         + [pltpu.SemaphoreType.DMA((blocks,))] * 2,
         compiler_params=pltpu.CompilerParams(collective_id=0, has_side_effects=True),
     )(
-        cycle_len, quad_weight, pair_wave.reshape(band_count, pair_dev), force,
+        cycle_len, quad_weight, pair_wave.reshape(1, -1), force,
         mixing.reshape(rows, levels), spectral, legendre,
     )
     return pl.pallas_call(

time: 31.9 us -> 33.5 us (1.050)
  Pallas kernels: 28.7 us -> 30.4 us
    pallas_call x1, Pallas kernels: 21.9 us -> 23.6 us  [on_device(): pl.pallas_call(functools.partial(grid_kernel, points_dev, lev_count, spli...]
where the time goes in v5:
time: 33.5 us; the launch traced here: 33.2 us
  Pallas kernels  30.4 us (91%)
  local copies, waits for them, and re-layouts  2.73 us (8%)
    pallas_call x1, Pallas kernels, on_device(): pl.pallas_call(functools.partial(grid_kernel, points_dev, lev_count, spli...  23.6 us
    pallas_call x1, Pallas kernels, on_device(): pl.pallas_call(functools.partial(direct_kernel, split), in_specs=[vmem, v...  6.8 us
    reshape x1, local copies, waits for them, and re-layouts, on_device(): pair_wave.reshape(1, -1)  1.29 us
    reshape x1, local copies, waits for them, and re-layouts, on_device(): forcing.reshape(rows, points_dev)  0.81 us

profile of v5, /device:TPU:0, one launch (start us, length us, event | category | flops | bytes accessed | tf_op | source)
XLA Modules:
  0.0 33.2 jit_solution(12620630632420419517)
XLA Ops:
  0.0 1.3 %reshape.9.low_ref = s32[1,1280]{1,0:T(1,128)} reshape(s32[1280]{0:T(1024)} %param.10) | data formatting | bytes 10240 | tf_op jit(solution)/shard_map/reshape | solution.py:367
  1.3 0.8 %reshape.10 = bf16[8,2564]{1,0:T(8,128)(2,1)S(1)} reshape(bf16[2,4,1,2564]{3,1,2,0:T(4,128)(2,1)} %param.12) | data formatting | bytes 82048 | tf_op jit(solution)/shard_map/reshape | solution.py:334
  2.1 0.6 %pad.4.forcing_ref = bf16[8,2816]{1,0:T(8,128)(2,1)} pad(bf16[8,2564]{1,0:T(8,128)(2,1)S(1)} %reshape.10, bf16[]{:T(256)} %constant.2.clone.1), padding=0_0x0_252 | pad | bytes 86082 | tf_op jit(solution)/shard_map/jit(_pad)/pad | solution.py:334
  2.7 23.6 %shard_map.73 = (f32[10,8,128]{2,1,0:T(8,128)}, s32[160,1]{1,0:T(8,128)}) custom-call(s32[8]{0:T(128)} %length_ref.1, f32[8]{0:T(128)} %weight_ref.1, s32[1,1280]{1,0:T(1,128)} %reshape.9.low_ref, bf16[8,2816]{1,0:T(8,128)(2,1)} %pad.4.forcing_ref, bf16[8,4]{1,0:T(8,128)(2,1)} %bitcast.3, bf16[2,2,1,160,2561]{4,3,2,1,0:T(8,128)(2,1)} %spec_hbm.1, ...), custom_call_target="tpu_custom_call" | custom-call | tf_op jit(solution)/shard_map/pallas_call | solution.py:341
  26.4 6.8 %shard_map.74 = bf16[2,2,1,160,2561]{4,3,2,1,0:T(8,128)(2,1)} custom-call(s32[160,1]{1,0:T(8,128)} %get-tuple-element.7.limit_ref, f32[10,8,128]{2,1,0:T(8,128)} %get-tuple-element.8.coeff_ref, bf16[160,8,2561]{2,1,0:T(8,128)(2,1)} %leg_hbm.3), custom_call_target="tpu_custom_call" | custom-call | tf_op jit(solution)/shard_map/pallas_call | solution.py:370

commit v6 on v4

--- a/solution.py
+++ b/solution.py
@@ -135,7 +135,10 @@
             barrier, inc=1, device_id={"band": band, "lev": lev}, device_id_type=pl.DeviceIdType.MESH
         )
 
-    parts = [low_ref[...], TRUNC - low_ref[...]]
+    own = blocks * pairs
+    line = low_ref[...].reshape(1, bands * own)
+    low = jnp.concatenate([line[:, k * own : (k + 1) * own] for k in range(bands)], axis=0)
+    parts = [low, TRUNC - low]
     if lanes > blocks * each:
         parts.append(jnp.full((bands, lanes - blocks * each), 1 << 14, jnp.int32))
     wave_ref[...] = jnp.concatenate(parts, axis=1)
@@ -253,7 +256,11 @@
         inside = (point < points_dev) & (base + point < length)
         cell = jnp.where(inside, grid[a * rows : (a + 1) * rows], 0.0)
         product = (cell[:levs] * cell[levs:]).astype(jnp.bfloat16).astype(jnp.float32)
-        total = cell + forcing_ref[:, a * INNER : (a + 1) * INNER].astype(jnp.float32)
+        force = forcing_ref[:, a * INNER : min((a + 1) * INNER, points_dev)].astype(jnp.float32)
+        if force.shape[1] < INNER:
+            rest = jnp.zeros((rows, INNER - force.shape[1]), jnp.float32)
+            force = jnp.concatenate([force, rest], axis=1)
+        total = cell + force
         for l2 in range(levs):
             total = total + mixing[:, l2 : l2 + 1] * product[l2 : l2 + 1]
         updated.append(jnp.where(inside, total, 0.0))
@@ -326,7 +333,7 @@
     waves = band_count * each_band
     used = pl.cdiv(points_dev, INNER)
     outer = pl.cdiv(used, 8) * 8
-    force = jnp.pad(forcing.reshape(rows, points_dev), ((0, 0), (0, used * INNER - points_dev)))
+    force = forcing.reshape(rows, points_dev)
     vmem = pl.BlockSpec(memory_space=pltpu.VMEM)
     smem = pl.BlockSpec(memory_space=pltpu.SMEM)
     slots = band_count * lev_count
@@ -359,7 +366,7 @@
         + [pltpu.SemaphoreType.DMA((blocks,))] * 2,
         compiler_params=pltpu.CompilerParams(collective_id=0, has_side_effects=True),
     )(
-        cycle_len, quad_weight, pair_wave.reshape(band_count, pair_dev), force,
+        cycle_len, quad_weight, pair_wave, force,
         mixing.reshape(rows, levels), spectral, legendre,
     )
     return pl.pallas_call(

time: 31.9 us -> 30.6 us (0.959)
  local copies, waits for them, and re-layouts: 2.8 us -> 1.42 us
    reshape x2 -> x1, local copies, waits for them, and re-layouts: 2.17 us -> 1.42 us  [on_device(): force = forcing.reshape(rows, points_dev)]
    pad x1 -> x0, local copies, waits for them, and re-layouts: 0.63 us -> none  [on_device(): jnp.pad(forcing.reshape(rows, points_dev), ((0, 0), (0, used * INNER - po...]
where the time goes in v6:
time: 30.6 us; the launch traced here: 30.3 us
  Pallas kernels  28.8 us (94%)
  local copies, waits for them, and re-layouts  1.42 us (5%)
    pallas_call x1, Pallas kernels, on_device(): pl.pallas_call(functools.partial(grid_kernel, points_dev, lev_count, spli...  22.1 us
    pallas_call x1, Pallas kernels, on_device(): pl.pallas_call(functools.partial(direct_kernel, split), in_specs=[vmem, v...  6.8 us
    reshape x1, local copies, waits for them, and re-layouts, on_device(): force = forcing.reshape(rows, points_dev)  1.42 us

profile of v6, /device:TPU:0, one launch (start us, length us, event | category | flops | bytes accessed | tf_op | source)
XLA Modules:
  0.0 30.3 jit_solution(6789300752920139797)
XLA Ops:
  0.0 1.4 %reshape.6.forcing_ref = bf16[8,2564]{1,0:T(8,128)(2,1)} reshape(bf16[2,4,1,2564]{3,1,2,0:T(4,128)(2,1)} %param.12) | data formatting | bytes 82048 | tf_op jit(solution)/shard_map/reshape | solution.py:336
  1.4 22.1 %shard_map.73 = (f32[10,8,128]{2,1,0:T(8,128)}, s32[160,1]{1,0:T(8,128)}) custom-call(s32[8]{0:T(128)} %length_ref.1, f32[8]{0:T(128)} %weight_ref.1, s32[1280]{0:T(1024)} %low_ref.1, bf16[8,2564]{1,0:T(8,128)(2,1)} %reshape.6.forcing_ref, bf16[8,4]{1,0:T(8,128)(2,1)} %bitcast.3, bf16[2,2,1,160,2561]{4,3,2,1,0:T(8,128)(2,1)} %spec_hbm.1, ...), custom_call_target="tpu_custom_call" | custom-call | tf_op jit(solution)/shard_map/pallas_call | solution.py:343
  23.5 6.8 %shard_map.74 = bf16[2,2,1,160,2561]{4,3,2,1,0:T(8,128)(2,1)} custom-call(s32[160,1]{1,0:T(8,128)} %get-tuple-element.7.limit_ref, f32[10,8,128]{2,1,0:T(8,128)} %get-tuple-element.8.coeff_ref, bf16[160,8,2561]{2,1,0:T(8,128)(2,1)} %leg_hbm.3), custom_call_target="tpu_custom_call" | custom-call | tf_op jit(solution)/shard_map/pallas_call | solution.py:372
